TPU v7x, 32 devices: a whole 2x2x4 slice. The times are simulated.
32 devices in a mesh: cand: 16 (over z, x, core), query: 2 (over y).
Axes of the slice: x: 2, y: 2, z: 4, core: 2. Of those that a mesh axis runs over, the one named last changes fastest.
Arguments:
- pool: bfloat16 [40960, 4096], P(('cand', 'query')), may hold values from -6 to 6
- cand_ids: int32 [32768], P(('cand', 'query')), may hold values from 0 to 1279
- pick_ids: int32 [32], P(('cand', 'query')), may hold values from 0 to 1279
- queries: bfloat16 [256, 4096], P('query'), may hold values from -6 to 6
Outputs:
- gains: float32 [32768], P(('cand', 'query'))
- coverage: float32 [256], P('query')
Inputs may be any that keep to these rules, and one draw needn't show every extreme that they name: `cand_ids`: each id is a row within the pool block of 1280 rows that lies on the same device as the id. `pick_ids`: each id is a row within the pool block of 1280 rows that lies on the same device as the id.
All inputs are finite; a program needn't handle non-finite values.
Results may differ from a plain program's by a relative error of at most 0.0003.
Values may be sent and summed in bfloat16 or wider, within the bound.
No kernel may reach another device: no remote copies, remote signals or barrier semaphores. Data moves between devices by JAX's collectives and lax.ppermute only.
A program may use at most 128 MiB of HBM per device.

v0:
```python
import functools
import math

import jax
import jax.numpy as jnp
from jax import lax
from jax.experimental import pallas as pl
from jax.experimental.pallas import tpu as pltpu
from jax.sharding import PartitionSpec as P

LANES = 128
SUBLANES = 8
CHUNKS = 2
OWN = 2
NT = (((1,), (1,)), ((), ()))
VMEM = pl.BlockSpec(memory_space=pltpu.VMEM)
SMEM = pl.BlockSpec(memory_space=pltpu.SMEM)
HBM = pl.BlockSpec(memory_space=pltpu.HBM)
PARAMS = pltpu.CompilerParams(vmem_limit_bytes=12 * 2**20)


def dot(rows, targets):
    return lax.dot_general(rows, targets, NT, preferred_element_type=jnp.float32)


def block_of(rows):
    return math.gcd(rows, 2 * LANES)


def cost(rows, count, width, read=0):
    return pl.CostEstimate(
        flops=2 * rows * max(count, 256) * width,
        bytes_accessed=rows * width * 2 + read,
        transcendentals=0,
    )


def start_kernel(share, pick_ids, pool, queries, *refs):
    picks, held, *pieces, tile, lines, pick_sem, sems = refs
    n_picks, cut, _ = picks.shape
    count, width = pieces[0].shape
    mine = pl.multiple_of(lax.rem(lax.axis_index("cand"), share) * count, count)
    moves = []
    for k, piece in enumerate(pieces):
        source = queries.at[pl.ds(mine, count), k * width : (k + 1) * width]
        moves.append(pltpu.make_async_copy(source, piece, sems.at[k]))
    moves.append(pltpu.make_async_copy(queries, held, sems.at[len(pieces)]))
    copies = []
    for i in range(n_picks):
        at = pl.multiple_of(pick_ids[i] // SUBLANES * SUBLANES, SUBLANES)
        copies.append(
            pltpu.make_async_copy(
                pool.at[pl.ds(at, SUBLANES), :], tile.at[i], pick_sem.at[i]
            )
        )
        copies[-1].start()
    for move in moves:
        move.start()
    row = lax.broadcasted_iota(jnp.int32, (SUBLANES, LANES), 0)
    for i in range(n_picks):
        copies[i].wait()
        own = row == pick_ids[i] % SUBLANES
        for c in range(cut):
            some = tile[i, :, c * LANES : (c + 1) * LANES].astype(jnp.float32)
            lines[c : c + 1, :] = jnp.sum(
                jnp.where(own, some, 0.0), axis=0, keepdims=True
            )
        picks[i] = lines[...].astype(jnp.bfloat16)
    for move in moves:
        move.wait()


def start(pool, pick_ids, queries, share):
    n_picks, depth = pick_ids.shape[0], pool.shape[1]
    piece = jax.ShapeDtypeStruct(
        (queries.shape[0] // share, depth // CHUNKS), queries.dtype
    )
    return pl.pallas_call(
        functools.partial(start_kernel, share),
        in_specs=[SMEM, HBM, HBM],
        out_specs=[VMEM] * (2 + CHUNKS),
        out_shape=[
            jax.ShapeDtypeStruct((n_picks, depth // LANES, LANES), pool.dtype),
            jax.ShapeDtypeStruct(queries.shape, queries.dtype),
        ]
        + [piece] * CHUNKS,
        scratch_shapes=[
            pltpu.VMEM((n_picks, SUBLANES, depth), pool.dtype),
            pltpu.VMEM((depth // LANES, LANES), jnp.float32),
            pltpu.SemaphoreType.DMA((n_picks,)),
            pltpu.SemaphoreType.DMA((CHUNKS + 1,)),
        ],
        compiler_params=PARAMS,
        cost_estimate=cost(0, 0, 0, 8 * pool.size),
        name="start",
    )(
        pick_ids,
        pltpu.with_memory_space_constraint(pool, pltpu.HBM),
        pltpu.with_memory_space_constraint(queries, pltpu.HBM),
    )


def scores_kernel(first, start, width, pool, *refs):
    targets, out = refs[:-1], refs[-1]
    targets = jnp.concatenate([t[...] for t in targets], axis=0)
    step = block_of(out.shape[0])
    for row in range(0, out.shape[0], step):
        out[row : row + step, :] = dot(
            pool[first + row : first + row + step, start : start + width], targets
        )


def scores(pool, targets, start, first, rows):
    width = targets[0].shape[1]
    count = sum(t.shape[0] for t in targets)
    return pl.pallas_call(
        functools.partial(scores_kernel, first, start, width),
        in_specs=[VMEM] * (1 + len(targets)),
        out_specs=VMEM,
        out_shape=jax.ShapeDtypeStruct((rows, count), jnp.float32),
        compiler_params=PARAMS,
        cost_estimate=cost(rows, count, width),
        name="scores",
    )(pool, *targets)


def gains_kernel(scale, sizes, groups, picks, ids, *refs):
    gains, cover, wide = refs[-3:]
    refs = list(refs[:-3])
    own = [refs.pop(0) for _ in sizes]
    parts, pieces = [], [[[refs.pop(0)]]]
    for n_parts, n_pieces in groups:
        parts.append([refs.pop(0) for _ in range(n_parts)])
        pieces.append([[refs.pop(0) for _ in range(n_pieces)] for _ in range(n_parts)])
    n_picks, cut, _ = picks.shape
    lines = math.gcd(cut, 4)
    width = lines * LANES

    wide[...] = picks[...].astype(jnp.float32).reshape(n_picks * cut, LANES)
    total = None
    for j in range(cut // lines):
        rows = jnp.concatenate(
            [
                wide[pl.ds(j * lines + k, n_picks, stride=cut), :]
                for k in range(lines)
            ],
            axis=1,
        ).astype(jnp.bfloat16)
        blocks = []
        for part in pieces:
            held = part[0][0].shape[1]
            part_of = part[(j * width) // held]
            at = (j * width) % held
            blocks += [piece[:, at : at + width] for piece in part_of]
        term = dot(rows, jnp.concatenate(blocks, axis=0))
        total = term if total is None else total + term
    best = jnp.max(total, axis=0, keepdims=True)
    covers, at = [], 0
    for count in [own[0].shape[1]] + [part[0].shape[1] for part in parts]:
        covers.append(best[:, at : at + count])
        at += count
    cover[...] = covers[0] * scale

    row = lax.broadcasted_iota(jnp.int32, (LANES, LANES), 0)
    lane = lax.broadcasted_iota(jnp.int32, (LANES, LANES), 1)
    diagonal = row == lane
    wanted = ids[...]
    block_wanted, lane_wanted = wanted // LANES, wanted % LANES
    found = jnp.zeros(wanted.shape, jnp.float32)
    block = 0
    for rows_of, size in zip(own, sizes):
        for k in range(size // LANES):
            some = slice(block * LANES, (block + 1) * LANES)
            every = [rows_of[k * LANES : (k + 1) * LANES, :]]
            for part in parts:
                s = part[0][some, :]
                for other in part[1:]:
                    s = s + other[some, :]
                every.append(s)
            above, highest = None, None
            for s, covered in zip(every, covers):
                over = jnp.maximum(s - covered, 0.0)
                above = over if above is None else above + over
                highest = s if highest is None else jnp.maximum(highest, s)
            gain = jnp.sum(above, axis=1, keepdims=True) + 1.0 * jnp.max(
                highest, axis=1, keepdims=True
            )
            line = jnp.sum(jnp.where(diagonal, gain, 0.0), axis=0, keepdims=True)
            table = jnp.broadcast_to(line, wanted.shape)
            here = jnp.take_along_axis(
                table, lane_wanted, axis=1, mode="promise_in_bounds"
            )
            found = jnp.where(block_wanted == block, here, found)
            block += 1
    gains[...] = found * scale


def gains_of(picks, ids, own, queries, blocks, scale):
    sizes = tuple(o.shape[0] for o in own)
    groups = tuple((len(parts), len(pieces[0])) for parts, pieces in blocks)
    flat = list(own) + [queries]
    for parts, pieces in blocks:
        flat += list(parts)
        for some in pieces:
            flat += list(some)
    n_picks, cut, _ = picks.shape
    return pl.pallas_call(
        functools.partial(gains_kernel, scale, sizes, groups),
        in_specs=[VMEM] * (2 + len(flat)),
        out_shape=(
            jax.ShapeDtypeStruct(ids.shape, jnp.float32),
            jax.ShapeDtypeStruct((1, queries.shape[0]), jnp.float32),
        ),
        scratch_shapes=[pltpu.VMEM((n_picks * cut, LANES), jnp.float32)],
        compiler_params=PARAMS,
        name="gains",
    )(picks, ids, *flat)


def strides(size):
    if size & (size - 1):
        return None
    return [size >> (k + 1) for k in range(size.bit_length() - 1)]


def gather_over(x, axis, size):
    if strides(size) is None:
        rest = [
            lax.ppermute(x, axis, [(i, (i + s) % size) for i in range(size)])
            for s in range(1, size)
        ]
        return jnp.concatenate([x] + rest, axis=0)
    for bit in strides(size):
        got = lax.ppermute(x, axis, [(i, i ^ bit) for i in range(size)])
        x = jnp.concatenate([x, got], axis=0)
    return x


def on_device(sizes, pool, cand_ids, pick_ids, queries):
    n_cand, n_query = sizes
    rows, depth = pool.shape
    scale = 1.0 / math.sqrt(depth)

    share = 2 if n_cand % 2 == 0 else 1
    width = depth // CHUNKS
    picks, held, *sent = start(pool, pick_ids, queries, share)
    picks = gather_over(picks, "query", n_query)
    picks = gather_over(picks, "cand", n_cand)

    own, first = [], 0
    for k in range(OWN):
        some = rows * (k + 1) // OWN // LANES * LANES - first
        own.append(scores(pool, [held], 0, first, some))
        first += some

    blocks = []
    for shift in range(1, n_query):
        parts, pieces = [], []
        for chunk in range(CHUNKS):
            got = lax.ppermute(
                sent[chunk],
                "query",
                [(i, (i + shift) % n_query) for i in range(n_query)],
            )
            both = [got]
            if share == 2:
                both.append(
                    lax.ppermute(got, "cand", [(i, i ^ 1) for i in range(n_cand)])
                )
            parts.append(scores(pool, both, chunk * width, 0, rows))
            pieces.append(both)
        blocks.append((parts, pieces))

    ids = cand_ids.reshape(-1, LANES)
    gains, cover = gains_of(picks, ids, own, held, blocks, scale)
    return gains.reshape(cand_ids.shape), cover.reshape(queries.shape[:1])


def solution(mesh):
    sizes = (mesh.shape["cand"], mesh.shape["query"])
    in_specs = (
        P(("cand", "query"), None),
        P(("cand", "query")),
        P(("cand", "query")),
        P("query", None),
    )
    out_specs = (P(("cand", "query")), P("query"))

    def body(*args):
        return on_device(sizes, *args)

    return jax.shard_map(
        body, mesh=mesh, in_specs=in_specs, out_specs=out_specs, check_vma=False
    )
```

profile of v0, /device:TPU:0, one launch (start us, length us, event | category | flops | bytes accessed | tf_op | source)
XLA Modules:
  0.0 29.8 jit_solution(8957516500100705958)
XLA Ops:
  0.6 0.0 copy-start
  1.4 1.6 %start.1 = (bf16[1,32,128]{2,1,0:T(8,128)(2,1)S(1)}, bf16[128,4096]{1,0:T(8,128)(2,1)S(1)}, bf16[64,2048]{1,0:T(8,128)(2,1)S(1)}, bf16[64,2048]{1,0:T(8,128)(2,1)S(1)}) custom-call(s32[1]{0:T(128)S(6)} %copy.15.pick_ids, bf16[1280,4096]{1,0:T(8,128)(2,1)} %pool.9, bf16[128,4096]{1,0:T(8,128)(2,1)} %queries.1), custom_call_target="tpu_custom_call" | custom-call | bytes 41943040 | tf_op jit(solution)/shard_map/start/pallas_call | solution.py:78
  3.0 3.1 %collective-permute-start = (bf16[1,32,128]{2,1,0:T(8,128)(2,1)S(1)}, bf16[1,32,128]{2,1,0:T(8,128)(2,1)S(1)}, u32[]{:S(2)}, u32[]{:S(2)}) collective-permute-start(bf16[1,32,128]{2,1,0:T(8,128)(2,1)S(1)} %get-tuple-element.8), channel_id=1, source_target_pairs={{0,1},{1,0},{2,3},{3,2},{4,5},{5,4},{6,7},{7,6},{8,9},{9,8},{10,11... | collective-permute-start | bytes 24584 | tf_op jit(solution)/shard_map/ppermute | solution.py:234
  6.1 0.1 collective-permute-start.5
  6.2 1.9 %collective-permute-start.7 = (bf16[64,2048]{1,0:T(8,128)(2,1)S(1)}, bf16[64,2048]{1,0:T(8,128)(2,1)S(1)}, u32[]{:S(2)}, u32[]{:S(2)}) collective-permute-start(bf16[64,2048]{1,0:T(8,128)(2,1)S(1)} %get-tuple-element.11), channel_id=1, source_target_pairs={{0,1},{1,0},{2,3},{3,2},{4,5},{5,4},{6,7},{7,6},{8,9},{9,8},{10,11... | collective-permute-start | bytes 786440 | tf_op jit(solution)/shard_map/ppermute | solution.py:260
  8.1 0.0 collective-permute-done
  8.1 2.7 %collective-permute-start.1 = (bf16[2,32,128]{2,1,0:T(8,128)(2,1)S(1)}, bf16[2,32,128]{2,1,0:T(8,128)(2,1)S(1)}, u32[]{:S(2)}, u32[]{:S(2)}) collective-permute-start(bf16[2,32,128]{2,1,0:T(8,128)(2,1)S(1)} %pad_maximum_fusion.2), channel_id=1, source_target_pairs={{0,16},{2,18},{4,20},{6,22},{8,24},{10,26},{12,28},{14,30},{16,0},... | collective-permute-start | bytes 49160 | tf_op jit(solution)/shard_map/ppermute | solution.py:234
  10.8 2.0 %collective-permute-done.1 = bf16[2,32,128]{2,1,0:T(8,128)(2,1)S(1)} collective-permute-done((bf16[2,32,128]{2,1,0:T(8,128)(2,1)S(1)}, bf16[2,32,128]{2,1,0:T(8,128)(2,1)S(1)}, u32[]{:S(2)}, u32[]{:S(2)}) %collective-permute-start.1) | collective-permute-done | bytes 16416 | tf_op jit(solution)/shard_map/ppermute | solution.py:234
  12.8 1.6 %collective-permute-start.2 = (bf16[4,32,128]{2,1,0:T(8,128)(2,1)S(1)}, bf16[4,32,128]{2,1,0:T(8,128)(2,1)S(1)}, u32[]{:S(2)}, u32[]{:S(2)}) collective-permute-start(bf16[4,32,128]{2,1,0:T(8,128)(2,1)S(1)} %pad_maximum_fusion.1), channel_id=1, source_target_pairs={{0,8},{2,10},{4,12},{6,14},{8,0},{10,2},{12,4},{14,6},{16,24},{18,... | collective-permute-start | bytes 98312 | tf_op jit(solution)/shard_map/ppermute | solution.py:234
  14.4 2.3 %collective-permute-done.2 = bf16[4,32,128]{2,1,0:T(8,128)(2,1)S(1)} collective-permute-done((bf16[4,32,128]{2,1,0:T(8,128)(2,1)S(1)}, bf16[4,32,128]{2,1,0:T(8,128)(2,1)S(1)}, u32[]{:S(2)}, u32[]{:S(2)}) %collective-permute-start.2) | collective-permute-done | bytes 32800 | tf_op jit(solution)/shard_map/ppermute | solution.py:234
  16.8 1.6 %collective-permute-start.3 = (bf16[8,32,128]{2,1,0:T(8,128)(2,1)S(1)}, bf16[8,32,128]{2,1,0:T(8,128)(2,1)S(1)}, u32[]{:S(2)}, u32[]{:S(2)}) collective-permute-start(bf16[8,32,128]{2,1,0:T(8,128)(2,1)S(1)} %pad_maximum_fusion), channel_id=1, source_target_pairs={{0,4},{2,6},{4,0},{6,2},{8,12},{10,14},{12,8},{14,10},{16,20},{18,... | collective-permute-start | bytes 196616 | tf_op jit(solution)/shard_map/ppermute | solution.py:234
  18.4 2.7 %collective-permute-done.3 = bf16[8,32,128]{2,1,0:T(8,128)(2,1)S(1)} collective-permute-done((bf16[8,32,128]{2,1,0:T(8,128)(2,1)S(1)}, bf16[8,32,128]{2,1,0:T(8,128)(2,1)S(1)}, u32[]{:S(2)}, u32[]{:S(2)}) %collective-permute-start.3) | collective-permute-done | bytes 65568 | tf_op jit(solution)/shard_map/ppermute | solution.py:234
  21.1 0.1 collective-permute-start.4
  21.2 0.0 collective-permute-done.7.refs_0_.refs_7_
  21.2 0.5 %collective-permute-start.8 = (bf16[64,2048]{1,0:T(8,128)(2,1)S(1)}, bf16[64,2048]{1,0:T(8,128)(2,1)S(1)}, u32[]{:S(2)}, u32[]{:S(2)}) collective-permute-start(bf16[64,2048]{1,0:T(8,128)(2,1)S(1)} %collective-permute-done.7.refs_0_.refs_7_), channel_id=1, source_target_pairs={{0,2},{2,0},{4,6},{6,4},{8,10},{10,8},{12,14},{14,12},{16,18},{18,... | collective-permute-start | bytes 786440 | tf_op jit(solution)/shard_map/ppermute | solution.py:268
  21.7 0.0 copy-done
  21.7 1.5 %scores.5.refs_1_ = f32[640,128]{1,0:T(8,128)S(1)} custom-call(bf16[1280,4096]{1,0:T(8,128)(2,1)S(1)} %copy-done, bf16[128,4096]{1,0:T(8,128)(2,1)S(1)} %get-tuple-element.9.refs_0_.refs_2_), custom_call_target="tpu_custom_call" | custom-call | flops 1342177280 | bytes 5242880 | tf_op jit(solution)/shard_map/scores/pallas_call | solution.py:116
  23.2 0.0 collective-permute-done.5.refs_0_.refs_5_
  23.2 0.1 collective-permute-start.6
  23.4 1.5 %scores.4.refs_0_ = f32[640,128]{1,0:T(8,128)S(1)} custom-call(bf16[1280,4096]{1,0:T(8,128)(2,1)S(1)} %copy-done, bf16[128,4096]{1,0:T(8,128)(2,1)S(1)} %get-tuple-element.9.refs_0_.refs_2_), custom_call_target="tpu_custom_call" | custom-call | flops 1342177280 | bytes 5242880 | tf_op jit(solution)/shard_map/scores/pallas_call | solution.py:116
  24.9 0.0 collective-permute-done.4
  24.9 0.0 copy-start.1
  24.9 0.0 collective-permute-done.8.refs_1_.refs_8_
  25.0 1.5 %scores.7.refs_4_ = f32[1280,128]{1,0:T(8,128)S(1)} custom-call(bf16[1280,4096]{1,0:T(8,128)(2,1)S(1)} %copy-done, bf16[64,2048]{1,0:T(8,128)(2,1)S(1)} %collective-permute-done.7.refs_0_.refs_7_, bf16[64,2048]{1,0:T(8,128)(2,1)S(1)} %collective-permute-done.8.refs_1_.refs_8_), custom_call_target="tpu_custom_call" | custom-call | flops 1342177280 | bytes 5242880 | tf_op jit(solution)/shard_map/scores/pallas_call | solution.py:116
  26.5 0.0 collective-permute-done.6.refs_1_.refs_6_
  26.5 1.5 %scores.6.refs_3_ = f32[1280,128]{1,0:T(8,128)S(1)} custom-call(bf16[1280,4096]{1,0:T(8,128)(2,1)S(1)} %copy-done, bf16[64,2048]{1,0:T(8,128)(2,1)S(1)} %collective-permute-done.5.refs_0_.refs_5_, bf16[64,2048]{1,0:T(8,128)(2,1)S(1)} %collective-permute-done.6.refs_1_.refs_6_), custom_call_target="tpu_custom_call" | custom-call | flops 1342177280 | bytes 5242880 | tf_op jit(solution)/shard_map/scores/pallas_call | solution.py:116
  28.0 0.0 copy-done.1
  28.0 1.8 %gains.1 = (f32[8,128]{1,0:T(8,128)}, f32[1,128]{1,0:T(1,128)}) custom-call(bf16[32,32,128]{2,1,0:T(8,128)(2,1)S(1)} %constant_dynamic-update-slice_fusion.5.picks, s32[8,128]{1,0:T(8,128)S(1)} %bitcast.3, f32[640,128]{1,0:T(8,128)S(1)} %scores.4.refs_0_, f32[640,128]{1,0:T(8,128)S(1)} %scores.5.refs_1_, ...), custom_call_target="tpu_custom_call" | custom-call | tf_op jit(solution)/shard_map/gains/pallas_call | solution.py:207
  (9 shorter events, 0.1 us)
Async XLA Ops:
  0.6 21.1 %copy-start = (bf16[1280,4096]{1,0:T(8,128)(2,1)S(1)}, bf16[1280,4096]{1,0:T(8,128)(2,1)}, u32[]{:S(2)}) copy-start(bf16[1280,4096]{1,0:T(8,128)(2,1)} %pool.9) | copy-start | bytes 31457284
  3.0 5.1 %collective-permute-start = (bf16[1,32,128]{2,1,0:T(8,128)(2,1)S(1)}, bf16[1,32,128]{2,1,0:T(8,128)(2,1)S(1)}, u32[]{:S(2)}, u32[]{:S(2)}) collective-permute-start(bf16[1,32,128]{2,1,0:T(8,128)(2,1)S(1)} %get-tuple-element.8), channel_id=1, source_target_pairs={{0,1},{1,0},{2,3},{3,2},{4,5},{5,4},{6,7},{7,6},{8,9},{9,8},{10,11... | collective-permute-start | bytes 24584 | tf_op jit(solution)/shard_map/ppermute | solution.py:234
  6.1 17.1 %collective-permute-start.5 = (bf16[64,2048]{1,0:T(8,128)(2,1)S(1)}, bf16[64,2048]{1,0:T(8,128)(2,1)S(1)}, u32[]{:S(2)}, u32[]{:S(2)}) collective-permute-start(bf16[64,2048]{1,0:T(8,128)(2,1)S(1)} %get-tuple-element.10), channel_id=1, source_target_pairs={{0,1},{1,0},{2,3},{3,2},{4,5},{5,4},{6,7},{7,6},{8,9},{9,8},{10,11... | collective-permute-start | bytes 786440 | tf_op jit(solution)/shard_map/ppermute | solution.py:260
  6.2 15.0 %collective-permute-start.7 = (bf16[64,2048]{1,0:T(8,128)(2,1)S(1)}, bf16[64,2048]{1,0:T(8,128)(2,1)S(1)}, u32[]{:S(2)}, u32[]{:S(2)}) collective-permute-start(bf16[64,2048]{1,0:T(8,128)(2,1)S(1)} %get-tuple-element.11), channel_id=1, source_target_pairs={{0,1},{1,0},{2,3},{3,2},{4,5},{5,4},{6,7},{7,6},{8,9},{9,8},{10,11... | collective-permute-start | bytes 786440 | tf_op jit(solution)/shard_map/ppermute | solution.py:260
  8.1 4.7 %collective-permute-start.1 = (bf16[2,32,128]{2,1,0:T(8,128)(2,1)S(1)}, bf16[2,32,128]{2,1,0:T(8,128)(2,1)S(1)}, u32[]{:S(2)}, u32[]{:S(2)}) collective-permute-start(bf16[2,32,128]{2,1,0:T(8,128)(2,1)S(1)} %pad_maximum_fusion.2), channel_id=1, source_target_pairs={{0,16},{2,18},{4,20},{6,22},{8,24},{10,26},{12,28},{14,30},{16,0},... | collective-permute-start | bytes 49160 | tf_op jit(solution)/shard_map/ppermute | solution.py:234
  12.8 3.9 %collective-permute-start.2 = (bf16[4,32,128]{2,1,0:T(8,128)(2,1)S(1)}, bf16[4,32,128]{2,1,0:T(8,128)(2,1)S(1)}, u32[]{:S(2)}, u32[]{:S(2)}) collective-permute-start(bf16[4,32,128]{2,1,0:T(8,128)(2,1)S(1)} %pad_maximum_fusion.1), channel_id=1, source_target_pairs={{0,8},{2,10},{4,12},{6,14},{8,0},{10,2},{12,4},{14,6},{16,24},{18,... | collective-permute-start | bytes 98312 | tf_op jit(solution)/shard_map/ppermute | solution.py:234
  16.8 4.3 %collective-permute-start.3 = (bf16[8,32,128]{2,1,0:T(8,128)(2,1)S(1)}, bf16[8,32,128]{2,1,0:T(8,128)(2,1)S(1)}, u32[]{:S(2)}, u32[]{:S(2)}) collective-permute-start(bf16[8,32,128]{2,1,0:T(8,128)(2,1)S(1)} %pad_maximum_fusion), channel_id=1, source_target_pairs={{0,4},{2,6},{4,0},{6,2},{8,12},{10,14},{12,8},{14,10},{16,20},{18,... | collective-permute-start | bytes 196616 | tf_op jit(solution)/shard_map/ppermute | solution.py:234
  21.1 3.8 %collective-permute-start.4 = (bf16[16,32,128]{2,1,0:T(8,128)(2,1)S(1)}, bf16[16,32,128]{2,1,0:T(8,128)(2,1)S(1)}, u32[]{:S(2)}, u32[]{:S(2)}) collective-permute-start(bf16[16,32,128]{2,1,0:T(8,128)(2,1)S(1)} %get-tuple-element.14), channel_id=1, source_target_pairs={{0,2},{2,0},{4,6},{6,4},{8,10},{10,8},{12,14},{14,12},{16,18},{18,... | collective-permute-start | bytes 393224 | tf_op jit(solution)/shard_map/ppermute | solution.py:234
  21.2 3.7 %collective-permute-start.8 = (bf16[64,2048]{1,0:T(8,128)(2,1)S(1)}, bf16[64,2048]{1,0:T(8,128)(2,1)S(1)}, u32[]{:S(2)}, u32[]{:S(2)}) collective-permute-start(bf16[64,2048]{1,0:T(8,128)(2,1)S(1)} %collective-permute-done.7.refs_0_.refs_7_), channel_id=1, source_target_pairs={{0,2},{2,0},{4,6},{6,4},{8,10},{10,8},{12,14},{14,12},{16,18},{18,... | collective-permute-start | bytes 786440 | tf_op jit(solution)/shard_map/ppermute | solution.py:268
  23.2 3.3 %collective-permute-start.6 = (bf16[64,2048]{1,0:T(8,128)(2,1)S(1)}, bf16[64,2048]{1,0:T(8,128)(2,1)S(1)}, u32[]{:S(2)}, u32[]{:S(2)}) collective-permute-start(bf16[64,2048]{1,0:T(8,128)(2,1)S(1)} %collective-permute-done.5.refs_0_.refs_5_), channel_id=1, source_target_pairs={{0,2},{2,0},{4,6},{6,4},{8,10},{10,8},{12,14},{14,12},{16,18},{18,... | collective-permute-start | bytes 786440 | tf_op jit(solution)/shard_map/ppermute | solution.py:268
  24.9 3.1 %copy-start.1 = (s32[1024]{0:T(1024)S(1)}, s32[1024]{0:T(1024)}, u32[]{:S(2)}) copy-start(s32[1024]{0:T(1024)} %param.5) | copy-start | bytes 12292
where the time goes:
time: 30 us; the launch traced here: 29.8 us
  starting transfers between devices  11.7 us (39%)
  Pallas kernels  9.39 us (31%)
  waiting for transfers between devices  7.05 us (24%)
  between operations  1.56 us (5%)
    ppermute x5, starting transfers between devices, gather_over(): got = lax.ppermute(x, axis, [(i, i ^ bit) for i in range(size)])  9.01 us
    ppermute x5, waiting for transfers between devices, gather_over(): got = lax.ppermute(x, axis, [(i, i ^ bit) for i in range(size)])  7.03 us
    pallas_call x4, Pallas kernels, scores(): pl.pallas_call(functools.partial(scores_kernel, first, start, width), in_...  6.04 us
    ppermute x2, starting transfers between devices, on_device(): lax.ppermute(sent[chunk], 'query', [(i, (i + shift) % n_query) for i in r...  2.03 us
    pallas_call x1, Pallas kernels, gains_of(): pl.pallas_call(functools.partial(gains_kernel, scale, sizes, groups), in_...  1.78 us
    pallas_call x1, Pallas kernels, start(): pl.pallas_call(functools.partial(start_kernel, share), in_specs=[SMEM, HB...  1.57 us
    ppermute x2, starting transfers between devices, on_device(): both.append(lax.ppermute(got, 'cand', [(i, i ^ 1) for i in range(n_cand)]))  0.64 us
  transfers between devices with their start and end apart: 9, of which 3 were waited for; matrix products, arithmetic and copies ran while one was open for 0% of the time, Pallas kernels for 15%

commit v1 on v0

v1 whole, which is shorter than its diff:
```python
import functools
import math

import jax
import jax.numpy as jnp
from jax import lax
from jax.experimental import pallas as pl
from jax.experimental.pallas import tpu as pltpu
from jax.sharding import PartitionSpec as P

LANES = 128
SUBLANES = 8
PARTS = (2, 1)
ROWS = 640
NT = (((1,), (1,)), ((), ()))
VMEM = pl.BlockSpec(memory_space=pltpu.VMEM)
HBM = pl.BlockSpec(memory_space=pltpu.HBM)
PARAMS = pltpu.CompilerParams(vmem_limit_bytes=12 * 2**20)


def dot(rows, targets):
    return lax.dot_general(rows, targets, NT, preferred_element_type=jnp.float32)


def cost(rows, count, width, read=0):
    return pl.CostEstimate(
        flops=2 * rows * max(count, 256) * width,
        bytes_accessed=rows * width * 2 + read,
        transcendentals=0,
    )


def start_kernel(share, pick_ids, pool, queries, *refs):
    picks, *pieces, tile, lines, pick_sem, sems = refs
    n_picks, cut, _ = picks.shape
    count = pieces[0].shape[0]
    wanted = [jnp.max(pick_ids[:, i : i + 1]) for i in range(n_picks)]
    copies = []
    for i in range(n_picks):
        at = pl.multiple_of(wanted[i] // SUBLANES * SUBLANES, SUBLANES)
        copies.append(
            pltpu.make_async_copy(
                pool.at[pl.ds(at, SUBLANES), :], tile.at[i], pick_sem.at[i]
            )
        )
        copies[-1].start()
    mine = pl.multiple_of(lax.rem(lax.axis_index("cand"), share) * count, count)
    moves, first = [], 0
    for k, piece in enumerate(pieces):
        source = queries.at[pl.ds(mine, count), first : first + piece.shape[1]]
        moves.append(pltpu.make_async_copy(source, piece, sems.at[k]))
        first += piece.shape[1]
    for move in moves:
        move.start()
    row = lax.broadcasted_iota(jnp.int32, (SUBLANES, LANES), 0)
    for i in range(n_picks):
        copies[i].wait()
        own = row == wanted[i] % SUBLANES
        for c in range(cut):
            some = tile[i, :, c * LANES : (c + 1) * LANES].astype(jnp.float32)
            lines[c : c + 1, :] = jnp.sum(
                jnp.where(own, some, 0.0), axis=0, keepdims=True
            )
        picks[i] = lines[...].astype(jnp.bfloat16)
    for move in moves:
        move.wait()


def chunks_of(depth):
    unit = LANES * math.gcd(depth // LANES, 4)
    first = depth * 5 // 8 // unit * unit
    return (first, depth - first)


def start(pool, pick_ids, queries, share):
    n_picks, depth = pick_ids.shape[0], pool.shape[1]
    widths = chunks_of(depth)
    return pl.pallas_call(
        functools.partial(start_kernel, share),
        in_specs=[VMEM, HBM, HBM],
        out_specs=[VMEM] * (1 + len(widths)),
        out_shape=[
            jax.ShapeDtypeStruct((n_picks, depth // LANES, LANES), pool.dtype),
        ]
        + [
            jax.ShapeDtypeStruct((queries.shape[0] // share, width), queries.dtype)
            for width in widths
        ],
        scratch_shapes=[
            pltpu.VMEM((n_picks, SUBLANES, depth), pool.dtype),
            pltpu.VMEM((depth // LANES, LANES), jnp.float32),
            pltpu.SemaphoreType.DMA((n_picks,)),
            pltpu.SemaphoreType.DMA((len(widths),)),
        ],
        compiler_params=PARAMS,
        cost_estimate=cost(0, 0, 0, 8 * pool.size),
        name="start",
    )(
        pick_ids.reshape(1, n_picks),
        pltpu.with_memory_space_constraint(pool, pltpu.HBM),
        pltpu.with_memory_space_constraint(queries, pltpu.HBM),
    )


def scores_kernel(first, start, width, pool, queries, *refs):
    pieces, out = refs[:-1], refs[-1]
    targets = [queries[:, start : start + width]] + [p[...] for p in pieces]
    targets = jnp.concatenate(targets, axis=0)
    step = math.gcd(out.shape[0], ROWS)
    for row in range(0, out.shape[0], step):
        out[row : row + step, :] = dot(
            pool[first + row : first + row + step, start : start + width], targets
        )


def scores(pool, queries, pieces, start, first, rows):
    width = pieces[0].shape[1] if pieces else queries.shape[1]
    count = queries.shape[0] + sum(p.shape[0] for p in pieces)
    return pl.pallas_call(
        functools.partial(scores_kernel, first, start, width),
        in_specs=[VMEM] * (2 + len(pieces)),
        out_specs=VMEM,
        out_shape=jax.ShapeDtypeStruct((rows, count), jnp.float32),
        compiler_params=PARAMS,
        cost_estimate=cost(rows, count, width),
        name="scores",
    )(pool, queries, *pieces)


def cover_kernel(groups, picks, *refs):
    best, wide = refs[-2:]
    refs = list(refs[:-2])
    blocks = [
        [[refs.pop(0) for _ in range(n_pieces)] for _ in range(n_chunks)]
        for n_chunks, n_pieces in groups
    ]
    n_picks, cut, _ = picks.shape
    lines = math.gcd(cut, 4)
    width = lines * LANES

    wide[...] = picks[...].astype(jnp.float32).reshape(n_picks * cut, LANES)
    total = None
    for j in range(cut // lines):
        rows = jnp.concatenate(
            [
                wide[pl.ds(j * lines + k, n_picks, stride=cut), :]
                for k in range(lines)
            ],
            axis=1,
        ).astype(jnp.bfloat16)
        some = []
        for block in blocks:
            at = j * width
            for pieces in block:
                held = pieces[0].shape[1]
                if 0 <= at < held:
                    some += [piece[:, at : at + width] for piece in pieces]
                at -= held
        term = dot(rows, jnp.concatenate(some, axis=0))
        total = term if total is None else total + term
    best[...] = jnp.max(total, axis=0, keepdims=True)


def cover_of(picks, blocks):
    groups = tuple((len(block), len(block[0])) for block in blocks)
    flat = [piece for block in blocks for pieces in block for piece in pieces]
    count = sum(piece.shape[0] for block in blocks for piece in block[0])
    n_picks, cut, _ = picks.shape
    return pl.pallas_call(
        functools.partial(cover_kernel, groups),
        in_specs=[VMEM] * (1 + len(flat)),
        out_specs=VMEM,
        out_shape=jax.ShapeDtypeStruct((1, count), jnp.float32),
        scratch_shapes=[pltpu.VMEM((n_picks * cut, LANES), jnp.float32)],
        compiler_params=PARAMS,
        cost_estimate=cost(2 * LANES, count, cut * LANES),
        name="cover",
    )(picks, *flat)


def gains_kernel(scale, n_bests, shape, ids, *refs):
    gains, cover = refs[-2:]
    refs = list(refs[:-2])
    best = refs.pop(0)[...]
    count = cover.shape[1]
    if n_bests == 2:
        theirs = refs.pop(0)[...]
        turned = [theirs[:, :count]]
        for at in range(count, best.shape[1], count):
            turned.append(pltpu.roll(theirs[:, at : at + count], count // 2, 1))
        best = jnp.maximum(best, jnp.concatenate(turned, axis=1))
    chunks = []
    for n_arrays in shape:
        lines = []
        for _ in range(n_arrays):
            ref = refs.pop(0)
            lines += [(ref, row) for row in range(0, ref.shape[0], LANES)]
        chunks.append(lines)
    cover[...] = best[:, :count] * scale

    row = lax.broadcasted_iota(jnp.int32, (LANES, LANES), 0)
    lane = lax.broadcasted_iota(jnp.int32, (LANES, LANES), 1)
    diagonal = row == lane
    wanted = ids[...]
    block_wanted, lane_wanted = wanted // LANES, wanted % LANES
    found = jnp.zeros(wanted.shape, jnp.float32)
    for block, every in enumerate(zip(*chunks)):
        above, highest = None, None
        for at in range(0, best.shape[1], LANES):
            some = slice(at, at + LANES)
            s = None
            for ref, first in every:
                term = ref[first : first + LANES, some]
                s = term if s is None else s + term
            over = jnp.maximum(s - best[:, some], 0.0)
            above = over if above is None else above + over
            highest = s if highest is None else jnp.maximum(highest, s)
        gain = jnp.sum(above, axis=1, keepdims=True) + 1.0 * jnp.max(
            highest, axis=1, keepdims=True
        )
        line = jnp.sum(jnp.where(diagonal, gain, 0.0), axis=0, keepdims=True)
        table = jnp.broadcast_to(line, wanted.shape)
        here = jnp.take_along_axis(table, lane_wanted, axis=1, mode="promise_in_bounds")
        found = jnp.where(block_wanted == block, here, found)
    gains[...] = found * scale


def gains_of(bests, ids, parts, count, scale):
    flat = bests + [p for part in parts for p in part]
    return pl.pallas_call(
        functools.partial(gains_kernel, scale, len(bests), tuple(map(len, parts))),
        in_specs=[VMEM] * (1 + len(flat)),
        out_shape=(
            jax.ShapeDtypeStruct(ids.shape, jnp.float32),
            jax.ShapeDtypeStruct((1, count), jnp.float32),
        ),
        compiler_params=PARAMS,
        name="gains",
    )(ids, *flat)


def strides(size):
    if size & (size - 1):
        return None
    return [size >> (k + 1) for k in range(size.bit_length() - 1)]


def gather_over(x, axis, size, least=1):
    if strides(size) is None:
        rest = [
            lax.ppermute(x, axis, [(i, (i + s) % size) for i in range(size)])
            for s in range(1, size)
        ]
        return jnp.concatenate([x] + rest, axis=0)
    for bit in strides(size):
        if bit >= least:
            got = lax.ppermute(x, axis, [(i, i ^ bit) for i in range(size)])
            x = jnp.concatenate([x, got], axis=0)
    return x


def on_device(sizes, pool, cand_ids, pick_ids, queries):
    n_cand, n_query = sizes
    rows, depth = pool.shape
    scale = 1.0 / math.sqrt(depth)
    mates = [(i, i ^ 1) for i in range(n_cand)]

    share = 2 if n_cand % 2 == 0 else 1
    picks, *sent = start(pool, pick_ids, queries, share)
    held = queries

    swapped = bool(strides(n_cand))
    picks = gather_over(picks, "query", n_query)
    picks = gather_over(picks, "cand", n_cand, 2 if swapped else 1)

    blocks = [[[held]]]
    for shift in range(1, n_query):
        block = []
        for piece in sent:
            got = lax.ppermute(
                piece,
                "query",
                [(i, (i + shift) % n_query) for i in range(n_query)],
            )
            both = [got]
            if share == 2:
                both.append(lax.ppermute(got, "cand", mates))
            block.append(both)
        blocks.append(block)

    parts, start_at = [], 0
    for chunk, piece in enumerate(sent):
        pieces = [p for block in blocks[1:] for p in block[chunk]]
        part, first = [], 0
        for k in range(PARTS[chunk]):
            some = rows * (k + 1) // PARTS[chunk] // LANES * LANES - first
            part.append(scores(pool, held, pieces, start_at, first, some))
            first += some
        parts.append(part)
        start_at += piece.shape[1]

    bests = [cover_of(picks, blocks)]
    if swapped:
        bests.append(lax.ppermute(bests[0], "cand", mates))
    gains, cover = gains_of(
        bests, cand_ids.reshape(-1, LANES), parts, queries.shape[0], scale
    )
    return gains.reshape(cand_ids.shape), cover.reshape(queries.shape[:1])


def solution(mesh):
    sizes = (mesh.shape["cand"], mesh.shape["query"])
    in_specs = (
        P(("cand", "query"), None),
        P(("cand", "query")),
        P(("cand", "query")),
        P("query", None),
    )
    out_specs = (P(("cand", "query")), P("query"))

    def body(*args):
        return on_device(sizes, *args)

    return jax.shard_map(
        body, mesh=mesh, in_specs=in_specs, out_specs=out_specs, check_vma=False
    )
```

time: 30 us -> 29.6 us (0.987)
  waiting for transfers between devices: 7.05 us -> 9.82 us
  Pallas kernels: 9.39 us -> 6.77 us
  starting transfers between devices: 11.7 us -> 11.2 us
    ppermute x4 -> x5, waiting for transfers between devices: 0.01 us -> 5.03 us  [the longest x2 5.02 us: on_device(): lax.ppermute(piece, 'query', [(i, (i + shift) % n_query) for i in range(n...]
    pallas_call x4 -> x3, Pallas kernels: 6.04 us -> 3.3 us  [scores(): pl.pallas_call(functools.partial(scores_kernel, first, start, width), in_...]
    ppermute x5 -> x4, waiting for transfers between devices: 7.03 us -> 4.79 us  [gather_over(): got = lax.ppermute(x, axis, [(i, i ^ bit) for i in range(size)])]
    ppermute x4 -> x5, starting transfers between devices: 2.67 us -> 2.33 us  [the longest x2 2.03 us: on_device(): lax.ppermute(piece, 'query', [(i, (i + shift) % n_query) for i in range(n...]
    pallas_call x2 -> x3, Pallas kernels: 3.35 us -> 3.47 us  [the longest x1 1.5 us: start(): pl.pallas_call(functools.partial(start_kernel, share), in_specs=[VMEM, HB...]
    ppermute x5 -> x4, starting transfers between devices: 9.01 us -> 8.91 us  [gather_over(): got = lax.ppermute(x, axis, [(i, i ^ bit) for i in range(size)])]
  transfers between devices with their start and end apart: 9 -> 9, of which waited for: 3 -> 3; matrix products, arithmetic and copies ran while one was open for 0% -> 0% of each run, Pallas kernels for 15% -> 11%
where the time goes in v1:
time: 29.6 us; the launch traced here: 29.4 us
  starting transfers between devices  11.2 us (38%)
  waiting for transfers between devices  9.82 us (33%)
  Pallas kernels  6.77 us (23%)
  between operations  1.55 us (5%)
    ppermute x4, starting transfers between devices, gather_over(): got = lax.ppermute(x, axis, [(i, i ^ bit) for i in range(size)])  8.91 us
    ppermute x2, waiting for transfers between devices, on_device(): lax.ppermute(piece, 'query', [(i, (i + shift) % n_query) for i in range(n...  5.02 us
    ppermute x4, waiting for transfers between devices, gather_over(): got = lax.ppermute(x, axis, [(i, i ^ bit) for i in range(size)])  4.79 us
    pallas_call x3, Pallas kernels, scores(): pl.pallas_call(functools.partial(scores_kernel, first, start, width), in_...  3.3 us
    ppermute x2, starting transfers between devices, on_device(): lax.ppermute(piece, 'query', [(i, (i + shift) % n_query) for i in range(n...  2.03 us
    pallas_call x1, Pallas kernels, start(): pl.pallas_call(functools.partial(start_kernel, share), in_specs=[VMEM, HB...  1.5 us
    pallas_call x1, Pallas kernels, gains_of(): pl.pallas_call(functools.partial(gains_kernel, scale, len(bests), tuple(m...  1.28 us
    pallas_call x1, Pallas kernels, cover_of(): pl.pallas_call(functools.partial(cover_kernel, groups), in_specs=[VMEM] *...  0.69 us
  transfers between devices with their start and end apart: 9, of which 3 were waited for; matrix products, arithmetic and copies ran while one was open for 0% of the time, Pallas kernels for 11%

profile of v1, /device:TPU:0, one launch (start us, length us, event | category | flops | bytes accessed | tf_op | source)
XLA Modules:
  0.0 29.4 jit_solution(14495057527282715908)
XLA Ops:
  0.6 0.0 copy-start.1
  0.6 0.0 copy-start
  1.4 1.5 %start.1 = (bf16[1,32,128]{2,1,0:T(8,128)(2,1)S(1)}, bf16[64,2560]{1,0:T(8,128)(2,1)S(1)}, bf16[64,1536]{1,0:T(8,128)(2,1)S(1)}) custom-call(s32[1,1]{1,0:T(1,128)} %bitcast.4.pick_ids, bf16[1280,4096]{1,0:T(8,128)(2,1)} %pool.7, bf16[128,4096]{1,0:T(8,128)(2,1)} %queries.7), custom_call_target="tpu_custom_call" | custom-call | bytes 41943040 | tf_op jit(solution)/shard_map/start/pallas_call | solution.py:78
  2.9 3.1 %collective-permute-start = (bf16[1,32,128]{2,1,0:T(8,128)(2,1)S(1)}, bf16[1,32,128]{2,1,0:T(8,128)(2,1)S(1)}, u32[]{:S(2)}, u32[]{:S(2)}) collective-permute-start(bf16[1,32,128]{2,1,0:T(8,128)(2,1)S(1)} %get-tuple-element.7), channel_id=1, source_target_pairs={{0,1},{1,0},{2,3},{3,2},{4,5},{5,4},{6,7},{7,6},{8,9},{9,8},{10,11... | collective-permute-start | bytes 24584 | tf_op jit(solution)/shard_map/ppermute | solution.py:257
  6.0 0.1 collective-permute-start.6
  6.1 1.9 %collective-permute-start.4 = (bf16[64,2560]{1,0:T(8,128)(2,1)S(1)}, bf16[64,2560]{1,0:T(8,128)(2,1)S(1)}, u32[]{:S(2)}, u32[]{:S(2)}) collective-permute-start(bf16[64,2560]{1,0:T(8,128)(2,1)S(1)} %get-tuple-element.8), channel_id=1, source_target_pairs={{0,1},{1,0},{2,3},{3,2},{4,5},{5,4},{6,7},{7,6},{8,9},{9,8},{10,11... | collective-permute-start | bytes 983048 | tf_op jit(solution)/shard_map/ppermute | solution.py:280
  8.0 0.0 collective-permute-done
  8.0 2.7 %collective-permute-start.1 = (bf16[2,32,128]{2,1,0:T(8,128)(2,1)S(1)}, bf16[2,32,128]{2,1,0:T(8,128)(2,1)S(1)}, u32[]{:S(2)}, u32[]{:S(2)}) collective-permute-start(bf16[2,32,128]{2,1,0:T(8,128)(2,1)S(1)} %pad_maximum_fusion.2), channel_id=1, source_target_pairs={{0,16},{2,18},{4,20},{6,22},{8,24},{10,26},{12,28},{14,30},{16,0},... | collective-permute-start | bytes 49160 | tf_op jit(solution)/shard_map/ppermute | solution.py:257
  10.7 2.0 %collective-permute-done.1 = bf16[2,32,128]{2,1,0:T(8,128)(2,1)S(1)} collective-permute-done((bf16[2,32,128]{2,1,0:T(8,128)(2,1)S(1)}, bf16[2,32,128]{2,1,0:T(8,128)(2,1)S(1)}, u32[]{:S(2)}, u32[]{:S(2)}) %collective-permute-start.1) | collective-permute-done | bytes 16416 | tf_op jit(solution)/shard_map/ppermute | solution.py:257
  12.8 1.6 %collective-permute-start.2 = (bf16[4,32,128]{2,1,0:T(8,128)(2,1)S(1)}, bf16[4,32,128]{2,1,0:T(8,128)(2,1)S(1)}, u32[]{:S(2)}, u32[]{:S(2)}) collective-permute-start(bf16[4,32,128]{2,1,0:T(8,128)(2,1)S(1)} %pad_maximum_fusion.1), channel_id=1, source_target_pairs={{0,8},{2,10},{4,12},{6,14},{8,0},{10,2},{12,4},{14,6},{16,24},{18,... | collective-permute-start | bytes 98312 | tf_op jit(solution)/shard_map/ppermute | solution.py:257
  14.4 5.0 %collective-permute-done.4.refs_1_.refs_0_ = bf16[64,2560]{1,0:T(8,128)(2,1)S(1)} collective-permute-done((bf16[64,2560]{1,0:T(8,128)(2,1)S(1)}, bf16[64,2560]{1,0:T(8,128)(2,1)S(1)}, u32[]{:S(2)}, u32[]{:S(2)}) %collective-permute-start.4) | collective-permute-done | bytes 327712 | tf_op jit(solution)/shard_map/ppermute | solution.py:280
  19.4 0.0 collective-permute-start.5
  19.4 0.0 collective-permute-done.2
  19.4 1.6 %collective-permute-start.3 = (bf16[8,32,128]{2,1,0:T(8,128)(2,1)S(1)}, bf16[8,32,128]{2,1,0:T(8,128)(2,1)S(1)}, u32[]{:S(2)}, u32[]{:S(2)}) collective-permute-start(bf16[8,32,128]{2,1,0:T(8,128)(2,1)S(1)} %pad_maximum_fusion), channel_id=1, source_target_pairs={{0,4},{2,6},{4,0},{6,2},{8,12},{10,14},{12,8},{14,10},{16,20},{18,... | collective-permute-start | bytes 196616 | tf_op jit(solution)/shard_map/ppermute | solution.py:257
  21.0 0.0 collective-permute-done.6.refs_3_.refs_0_
  21.0 0.2 collective-permute-start.7
  21.2 2.8 %collective-permute-done.3 = bf16[8,32,128]{2,1,0:T(8,128)(2,1)S(1)} collective-permute-done((bf16[8,32,128]{2,1,0:T(8,128)(2,1)S(1)}, bf16[8,32,128]{2,1,0:T(8,128)(2,1)S(1)}, u32[]{:S(2)}, u32[]{:S(2)}) %collective-permute-start.3) | collective-permute-done | bytes 65568 | tf_op jit(solution)/shard_map/ppermute | solution.py:257
  24.0 0.0 collective-permute-done.7.refs_4_.refs_1_
  24.0 0.0 copy-done.1
  24.0 0.0 copy-done
  24.0 1.2 %scores.5.refs_4_ = f32[1280,256]{1,0:T(8,128)S(1)} custom-call(bf16[1280,4096]{1,0:T(8,128)(2,1)S(1)} %copy-done, bf16[128,4096]{1,0:T(8,128)(2,1)S(1)} %copy-done.1, bf16[64,1536]{1,0:T(8,128)(2,1)S(1)} %collective-permute-done.6.refs_3_.refs_0_, bf16[64,1536]{1,0:T(8,128)(2,1)S(1)} %collective-permute-done.7.refs_4_.refs_1_), custom_call_target="tpu_custom_call" | custom-call | flops 1006632960 | bytes 3932160 | tf_op jit(solution)/shard_map/scores/pallas_call | solution.py:119
  25.2 0.0 collective-permute-done.5.refs_2_.refs_1_
  25.2 0.7 %cover.1.refs_0_ = f32[1,256]{1,0:T(1,128)S(1)} custom-call(bf16[16,32,128]{2,1,0:T(8,128)(2,1)S(1)} %constant_dynamic-update-slice_fusion.picks, bf16[128,4096]{1,0:T(8,128)(2,1)S(1)} %copy-done.1, bf16[64,2560]{1,0:T(8,128)(2,1)S(1)} %collective-permute-done.4.refs_1_.refs_0_, bf16[64,2560]{1,0:T(8,128)(2,1)S(1)} %collective-permute-done.5.refs_2_.refs_1_, ...), custom_call_target="tpu_custom_call" | custom-call | flops 536870912 | bytes 2097152 | tf_op jit(solution)/shard_map/cover/pallas_call | solution.py:169
  26.0 0.0 copy-start.2
  26.0 0.1 collective-permute-start.8
  26.0 1.0 %scores.4.refs_3_ = f32[640,256]{1,0:T(8,128)S(1)} custom-call(bf16[1280,4096]{1,0:T(8,128)(2,1)S(1)} %copy-done, bf16[128,4096]{1,0:T(8,128)(2,1)S(1)} %copy-done.1, bf16[64,2560]{1,0:T(8,128)(2,1)S(1)} %collective-permute-done.4.refs_1_.refs_0_, bf16[64,2560]{1,0:T(8,128)(2,1)S(1)} %collective-permute-done.5.refs_2_.refs_1_), custom_call_target="tpu_custom_call" | custom-call | flops 838860800 | bytes 3276800 | tf_op jit(solution)/shard_map/scores/pallas_call | solution.py:119
  27.1 1.0 %scores.3.refs_2_ = f32[640,256]{1,0:T(8,128)S(1)} custom-call(bf16[1280,4096]{1,0:T(8,128)(2,1)S(1)} %copy-done, bf16[128,4096]{1,0:T(8,128)(2,1)S(1)} %copy-done.1, bf16[64,2560]{1,0:T(8,128)(2,1)S(1)} %collective-permute-done.4.refs_1_.refs_0_, bf16[64,2560]{1,0:T(8,128)(2,1)S(1)} %collective-permute-done.5.refs_2_.refs_1_), custom_call_target="tpu_custom_call" | custom-call | flops 838860800 | bytes 3276800 | tf_op jit(solution)/shard_map/scores/pallas_call | solution.py:119
  28.1 0.0 collective-permute-done.8.refs_1_
  28.2 0.0 copy-done.2
  28.2 1.3 %gains.1 = (f32[8,128]{1,0:T(8,128)}, f32[1,128]{1,0:T(1,128)}) custom-call(s32[8,128]{1,0:T(8,128)S(1)} %bitcast.5, f32[1,256]{1,0:T(1,128)S(1)} %cover.1.refs_0_, f32[1,256]{1,0:T(1,128)S(1)} %collective-permute-done.8.refs_1_, f32[640,256]{1,0:T(8,128)S(1)} %scores.3.refs_2_, f32[640,256]{1,0:T(8,128)S(1)} %scores.4.refs_3_, f32[1280,256]{1,0:T(8,128)S(1)} %scores.5.refs_4_), custom_call_target="tpu_custom_call" | custom-call | tf_op jit(solution)/shard_map/gains/pallas_call | solution.py:230
  (8 shorter events, 0.1 us)
Async XLA Ops:
  0.6 23.4 %copy-start.1 = (bf16[128,4096]{1,0:T(8,128)(2,1)S(1)}, bf16[128,4096]{1,0:T(8,128)(2,1)}, u32[]{:S(2)}) copy-start(bf16[128,4096]{1,0:T(8,128)(2,1)} %queries.7) | copy-start | bytes 3145732
  0.6 23.4 %copy-start = (bf16[1280,4096]{1,0:T(8,128)(2,1)S(1)}, bf16[1280,4096]{1,0:T(8,128)(2,1)}, u32[]{:S(2)}) copy-start(bf16[1280,4096]{1,0:T(8,128)(2,1)} %pool.7) | copy-start | bytes 31457284
  2.9 5.1 %collective-permute-start = (bf16[1,32,128]{2,1,0:T(8,128)(2,1)S(1)}, bf16[1,32,128]{2,1,0:T(8,128)(2,1)S(1)}, u32[]{:S(2)}, u32[]{:S(2)}) collective-permute-start(bf16[1,32,128]{2,1,0:T(8,128)(2,1)S(1)} %get-tuple-element.7), channel_id=1, source_target_pairs={{0,1},{1,0},{2,3},{3,2},{4,5},{5,4},{6,7},{7,6},{8,9},{9,8},{10,11... | collective-permute-start | bytes 24584 | tf_op jit(solution)/shard_map/ppermute | solution.py:257
  6.0 15.0 %collective-permute-start.6 = (bf16[64,1536]{1,0:T(8,128)(2,1)S(1)}, bf16[64,1536]{1,0:T(8,128)(2,1)S(1)}, u32[]{:S(2)}, u32[]{:S(2)}) collective-permute-start(bf16[64,1536]{1,0:T(8,128)(2,1)S(1)} %get-tuple-element.9), channel_id=1, source_target_pairs={{0,1},{1,0},{2,3},{3,2},{4,5},{5,4},{6,7},{7,6},{8,9},{9,8},{10,11... | collective-permute-start | bytes 589832 | tf_op jit(solution)/shard_map/ppermute | solution.py:280
  6.1 13.3 %collective-permute-start.4 = (bf16[64,2560]{1,0:T(8,128)(2,1)S(1)}, bf16[64,2560]{1,0:T(8,128)(2,1)S(1)}, u32[]{:S(2)}, u32[]{:S(2)}) collective-permute-start(bf16[64,2560]{1,0:T(8,128)(2,1)S(1)} %get-tuple-element.8), channel_id=1, source_target_pairs={{0,1},{1,0},{2,3},{3,2},{4,5},{5,4},{6,7},{7,6},{8,9},{9,8},{10,11... | collective-permute-start | bytes 983048 | tf_op jit(solution)/shard_map/ppermute | solution.py:280
  8.0 4.7 %collective-permute-start.1 = (bf16[2,32,128]{2,1,0:T(8,128)(2,1)S(1)}, bf16[2,32,128]{2,1,0:T(8,128)(2,1)S(1)}, u32[]{:S(2)}, u32[]{:S(2)}) collective-permute-start(bf16[2,32,128]{2,1,0:T(8,128)(2,1)S(1)} %pad_maximum_fusion.2), channel_id=1, source_target_pairs={{0,16},{2,18},{4,20},{6,22},{8,24},{10,26},{12,28},{14,30},{16,0},... | collective-permute-start | bytes 49160 | tf_op jit(solution)/shard_map/ppermute | solution.py:257
  12.8 6.6 %collective-permute-start.2 = (bf16[4,32,128]{2,1,0:T(8,128)(2,1)S(1)}, bf16[4,32,128]{2,1,0:T(8,128)(2,1)S(1)}, u32[]{:S(2)}, u32[]{:S(2)}) collective-permute-start(bf16[4,32,128]{2,1,0:T(8,128)(2,1)S(1)} %pad_maximum_fusion.1), channel_id=1, source_target_pairs={{0,8},{2,10},{4,12},{6,14},{8,0},{10,2},{12,4},{14,6},{16,24},{18,... | collective-permute-start | bytes 98312 | tf_op jit(solution)/shard_map/ppermute | solution.py:257
  19.4 5.8 %collective-permute-start.5 = (bf16[64,2560]{1,0:T(8,128)(2,1)S(1)}, bf16[64,2560]{1,0:T(8,128)(2,1)S(1)}, u32[]{:S(2)}, u32[]{:S(2)}) collective-permute-start(bf16[64,2560]{1,0:T(8,128)(2,1)S(1)} %collective-permute-done.4.refs_1_.refs_0_), channel_id=1, source_target_pairs={{0,2},{2,0},{4,6},{6,4},{8,10},{10,8},{12,14},{14,12},{16,18},{18,... | collective-permute-start | bytes 983048 | tf_op jit(solution)/shard_map/ppermute | solution.py:287
  19.4 4.6 %collective-permute-start.3 = (bf16[8,32,128]{2,1,0:T(8,128)(2,1)S(1)}, bf16[8,32,128]{2,1,0:T(8,128)(2,1)S(1)}, u32[]{:S(2)}, u32[]{:S(2)}) collective-permute-start(bf16[8,32,128]{2,1,0:T(8,128)(2,1)S(1)} %pad_maximum_fusion), channel_id=1, source_target_pairs={{0,4},{2,6},{4,0},{6,2},{8,12},{10,14},{12,8},{14,10},{16,20},{18,... | collective-permute-start | bytes 196616 | tf_op jit(solution)/shard_map/ppermute | solution.py:257
  21.0 3.0 %collective-permute-start.7 = (bf16[64,1536]{1,0:T(8,128)(2,1)S(1)}, bf16[64,1536]{1,0:T(8,128)(2,1)S(1)}, u32[]{:S(2)}, u32[]{:S(2)}) collective-permute-start(bf16[64,1536]{1,0:T(8,128)(2,1)S(1)} %collective-permute-done.6.refs_3_.refs_0_), channel_id=1, source_target_pairs={{0,2},{2,0},{4,6},{6,4},{8,10},{10,8},{12,14},{14,12},{16,18},{18,... | collective-permute-start | bytes 589832 | tf_op jit(solution)/shard_map/ppermute | solution.py:287
  26.0 2.2 %copy-start.2 = (s32[1024]{0:T(1024)S(1)}, s32[1024]{0:T(1024)}, u32[]{:S(2)}) copy-start(s32[1024]{0:T(1024)} %param.5) | copy-start | bytes 12292
  26.0 2.2 %collective-permute-start.8 = (f32[1,256]{1,0:T(1,128)S(1)}, f32[1,256]{1,0:T(1,128)S(1)}, u32[]{:S(2)}, u32[]{:S(2)}) collective-permute-start(f32[1,256]{1,0:T(1,128)S(1)} %cover.1.refs_0_), channel_id=1, source_target_pairs={{0,2},{2,0},{4,6},{6,4},{8,10},{10,8},{12,14},{14,12},{16,18},{18,... | collective-permute-start | bytes 3080 | tf_op jit(solution)/shard_map/ppermute | solution.py:304

commit v2 on v1

--- a/solution.py
+++ b/solution.py
@@ -10,7 +10,7 @@
 
 LANES = 128
 SUBLANES = 8
-PARTS = (2, 1)
+PARTS = 2
 ROWS = 640
 NT = (((1,), (1,)), ((), ()))
 VMEM = pl.BlockSpec(memory_space=pltpu.VMEM)
@@ -34,7 +34,7 @@
     picks, *pieces, tile, lines, pick_sem, sems = refs
     n_picks, cut, _ = picks.shape
     count = pieces[0].shape[0]
-    wanted = [jnp.max(pick_ids[:, i : i + 1]) for i in range(n_picks)]
+    wanted = [pick_ids[i] for i in range(n_picks)]
     copies = []
     for i in range(n_picks):
         at = pl.multiple_of(wanted[i] // SUBLANES * SUBLANES, SUBLANES)
@@ -77,7 +77,7 @@
     widths = chunks_of(depth)
     return pl.pallas_call(
         functools.partial(start_kernel, share),
-        in_specs=[VMEM, HBM, HBM],
+        in_specs=[pl.BlockSpec(memory_space=pltpu.SMEM), HBM, HBM],
         out_specs=[VMEM] * (1 + len(widths)),
         out_shape=[
             jax.ShapeDtypeStruct((n_picks, depth // LANES, LANES), pool.dtype),
@@ -96,16 +96,22 @@
         cost_estimate=cost(0, 0, 0, 8 * pool.size),
         name="start",
     )(
-        pick_ids.reshape(1, n_picks),
+        pick_ids,
         pltpu.with_memory_space_constraint(pool, pltpu.HBM),
         pltpu.with_memory_space_constraint(queries, pltpu.HBM),
     )
 
 
+def targets_of(queries, pieces, start):
+    width = pieces[0].shape[1] if pieces else queries.shape[1]
+    return jnp.concatenate(
+        [queries[:, start : start + width]] + [p[...] for p in pieces], axis=0
+    )
+
+
 def scores_kernel(first, start, width, pool, queries, *refs):
     pieces, out = refs[:-1], refs[-1]
-    targets = [queries[:, start : start + width]] + [p[...] for p in pieces]
-    targets = jnp.concatenate(targets, axis=0)
+    targets = targets_of(queries, pieces, start)
     step = math.gcd(out.shape[0], ROWS)
     for row in range(0, out.shape[0], step):
         out[row : row + step, :] = dot(
@@ -125,6 +131,52 @@
         cost_estimate=cost(rows, count, width),
         name="scores",
     )(pool, queries, *pieces)
+
+
+def diagonal():
+    row = lax.broadcasted_iota(jnp.int32, (LANES, LANES), 0)
+    return row == lax.broadcasted_iota(jnp.int32, (LANES, LANES), 1)
+
+
+def in_line(column, keep):
+    return jnp.sum(jnp.where(keep, column, 0.0), axis=0, keepdims=True)
+
+
+def totals_kernel(start, width, n_before, pool, queries, *refs):
+    before, pieces = refs[:n_before], refs[n_before:-2]
+    out, top = refs[-2:]
+    targets = targets_of(queries, pieces, start)
+    keep = diagonal()
+    first = 0
+    for ref in before:
+        step = math.gcd(ref.shape[0], ROWS)
+        for row in range(0, ref.shape[0], step):
+            at = first + row
+            last = dot(pool[at : at + step, start : start + width], targets)
+            for k in range(0, step, LANES):
+                s = ref[row + k : row + k + LANES, :] + last[k : k + LANES, :]
+                out[at + k : at + k + LANES, :] = s
+                highest = jnp.max(s, axis=1, keepdims=True)
+                block = (at + k) // LANES
+                top[block : block + 1, :] = in_line(highest, keep)
+        first += ref.shape[0]
+
+
+def totals(pool, queries, before, pieces, start):
+    width = pieces[0].shape[1] if pieces else queries.shape[1]
+    rows, count = sum(b.shape[0] for b in before), before[0].shape[1]
+    return pl.pallas_call(
+        functools.partial(totals_kernel, start, width, len(before)),
+        in_specs=[VMEM] * (2 + len(before) + len(pieces)),
+        out_specs=[VMEM, VMEM],
+        out_shape=[
+            jax.ShapeDtypeStruct((rows, count), jnp.float32),
+            jax.ShapeDtypeStruct((rows // LANES, LANES), jnp.float32),
+        ],
+        compiler_params=PARAMS,
+        cost_estimate=cost(rows, count, width),
+        name="totals",
+    )(pool, queries, *before, *pieces)
 
 
 def cover_kernel(groups, picks, *refs):
@@ -178,84 +230,72 @@
     )(picks, *flat)
 
 
-def gains_kernel(scale, n_bests, shape, ids, *refs):
-    gains, cover = refs[-2:]
-    refs = list(refs[:-2])
-    best = refs.pop(0)[...]
+def gains_kernel(scale, ids, total, top, *refs):
+    bests, (gains, cover) = refs[:-2], refs[-2:]
+    best = bests[0][...]
     count = cover.shape[1]
-    if n_bests == 2:
-        theirs = refs.pop(0)[...]
+    if len(bests) == 2:
+        theirs = bests[1][...]
         turned = [theirs[:, :count]]
         for at in range(count, best.shape[1], count):
             turned.append(pltpu.roll(theirs[:, at : at + count], count // 2, 1))
         best = jnp.maximum(best, jnp.concatenate(turned, axis=1))
-    chunks = []
-    for n_arrays in shape:
-        lines = []
-        for _ in range(n_arrays):
-            ref = refs.pop(0)
-            lines += [(ref, row) for row in range(0, ref.shape[0], LANES)]
-        chunks.append(lines)
     cover[...] = best[:, :count] * scale
 
-    row = lax.broadcasted_iota(jnp.int32, (LANES, LANES), 0)
-    lane = lax.broadcasted_iota(jnp.int32, (LANES, LANES), 1)
-    diagonal = row == lane
+    keep = diagonal()
     wanted = ids[...]
     block_wanted, lane_wanted = wanted // LANES, wanted % LANES
     found = jnp.zeros(wanted.shape, jnp.float32)
-    for block, every in enumerate(zip(*chunks)):
-        above, highest = None, None
-        for at in range(0, best.shape[1], LANES):
-            some = slice(at, at + LANES)
-            s = None
-            for ref, first in every:
-                term = ref[first : first + LANES, some]
-                s = term if s is None else s + term
-            over = jnp.maximum(s - best[:, some], 0.0)
-            above = over if above is None else above + over
-            highest = s if highest is None else jnp.maximum(highest, s)
-        gain = jnp.sum(above, axis=1, keepdims=True) + 1.0 * jnp.max(
-            highest, axis=1, keepdims=True
-        )
-        line = jnp.sum(jnp.where(diagonal, gain, 0.0), axis=0, keepdims=True)
+    for block in range(top.shape[0]):
+        s = total[block * LANES : (block + 1) * LANES, :]
+        above = jnp.sum(jnp.maximum(s - best, 0.0), axis=1, keepdims=True)
+        line = in_line(above, keep) + 1.0 * top[block : block + 1, :]
         table = jnp.broadcast_to(line, wanted.shape)
         here = jnp.take_along_axis(table, lane_wanted, axis=1, mode="promise_in_bounds")
         found = jnp.where(block_wanted == block, here, found)
     gains[...] = found * scale
 
 
-def gains_of(bests, ids, parts, count, scale):
-    flat = bests + [p for part in parts for p in part]
-    return pl.pallas_call(
-        functools.partial(gains_kernel, scale, len(bests), tuple(map(len, parts))),
-        in_specs=[VMEM] * (1 + len(flat)),
+def gains_of(bests, ids, total, top, count, scale):
+    return pl.pallas_call(
+        functools.partial(gains_kernel, scale),
+        in_specs=[VMEM] * (3 + len(bests)),
         out_shape=(
             jax.ShapeDtypeStruct(ids.shape, jnp.float32),
             jax.ShapeDtypeStruct((1, count), jnp.float32),
         ),
         compiler_params=PARAMS,
         name="gains",
-    )(ids, *flat)
-
-
-def strides(size):
-    if size & (size - 1):
-        return None
-    return [size >> (k + 1) for k in range(size.bit_length() - 1)]
-
-
-def gather_over(x, axis, size, least=1):
-    if strides(size) is None:
+    )(ids, total, top, *bests)
+
+
+def is_power(size):
+    return size & (size - 1) == 0
+
+
+def stages(n_cand, n_query):
+    n = n_cand * n_query
+    bits = [1 << k for k in range(n.bit_length() - 1) if 1 << k != n_query]
+    rounds = [[bit] for bit in bits]
+    if len(bits) > 1:
+        low, high = bits[-2:]
+        rounds[-2:] = [[low | high, high, low]]
+    return rounds
+
+
+def gather_over(x, n_cand, n_query, swapped):
+    both, n = ("cand", "query"), n_cand * n_query
+    if not swapped:
         rest = [
-            lax.ppermute(x, axis, [(i, (i + s) % size) for i in range(size)])
-            for s in range(1, size)
+            lax.ppermute(x, both, [(i, (i + s) % n) for i in range(n)])
+            for s in range(1, n)
         ]
         return jnp.concatenate([x] + rest, axis=0)
-    for bit in strides(size):
-        if bit >= least:
-            got = lax.ppermute(x, axis, [(i, i ^ bit) for i in range(size)])
-            x = jnp.concatenate([x, got], axis=0)
+    for masks in stages(n_cand, n_query):
+        got = []
+        for mask in masks:
+            got.append(lax.ppermute(x, both, [(i, i ^ mask) for i in range(n)]))
+        x = jnp.concatenate([x] + got, axis=0)
     return x
 
 
@@ -269,9 +309,8 @@
     picks, *sent = start(pool, pick_ids, queries, share)
     held = queries
 
-    swapped = bool(strides(n_cand))
-    picks = gather_over(picks, "query", n_query)
-    picks = gather_over(picks, "cand", n_cand, 2 if swapped else 1)
+    swapped = n_cand > 1 and is_power(n_cand) and is_power(n_query)
+    picks = gather_over(picks, n_cand, n_query, swapped)
 
     blocks = [[[held]]]
     for shift in range(1, n_query):
@@ -288,22 +327,20 @@
             block.append(both)
         blocks.append(block)
 
-    parts, start_at = [], 0
-    for chunk, piece in enumerate(sent):
-        pieces = [p for block in blocks[1:] for p in block[chunk]]
-        part, first = [], 0
-        for k in range(PARTS[chunk]):
-            some = rows * (k + 1) // PARTS[chunk] // LANES * LANES - first
-            part.append(scores(pool, held, pieces, start_at, first, some))
-            first += some
-        parts.append(part)
-        start_at += piece.shape[1]
+    pieces = [p for block in blocks[1:] for p in block[0]]
+    before, first = [], 0
+    for k in range(PARTS):
+        some = rows * (k + 1) // PARTS // LANES * LANES - first
+        before.append(scores(pool, held, pieces, 0, first, some))
+        first += some
+    pieces = [p for block in blocks[1:] for p in block[1]]
+    total, top = totals(pool, held, before, pieces, sent[0].shape[1])
 
     bests = [cover_of(picks, blocks)]
     if swapped:
         bests.append(lax.ppermute(bests[0], "cand", mates))
     gains, cover = gains_of(
-        bests, cand_ids.reshape(-1, LANES), parts, queries.shape[0], scale
+        bests, cand_ids.reshape(-1, LANES), total, top, queries.shape[0], scale
     )
     return gains.reshape(cand_ids.shape), cover.reshape(queries.shape[:1])
 

time: 29.6 us -> 26.9 us (0.909)
  waiting for transfers between devices: 9.82 us -> 6.58 us
  starting transfers between devices: 11.2 us -> 11.9 us
    ppermute x4 -> x5, waiting for transfers between devices: 4.79 us -> 2.6 us  [gather_over(): got.append(lax.ppermute(x, both, [(i, i ^ mask) for i in range(n)]))]
    ppermute x2, waiting for transfers between devices: 5.02 us -> 3.07 us  [on_device(): lax.ppermute(piece, 'query', [(i, (i + shift) % n_query) for i in range(n...]
    pallas_call x3 -> x2, Pallas kernels: 3.3 us -> 2.09 us  [scores(): pl.pallas_call(functools.partial(scores_kernel, first, start, width), in_...]
    pallas_call x2 -> x3, Pallas kernels: 2.77 us -> 3.87 us  [the longest x1 1.47 us: start(): pl.pallas_call(functools.partial(start_kernel, share), in_specs=[pl.Block...]
    ppermute x2, waiting for transfers between devices: 0.01 us -> 0.9 us  [on_device(): both.append(lax.ppermute(got, 'cand', mates))]
    ppermute x2, starting transfers between devices: 0.23 us -> 0.57 us  [on_device(): both.append(lax.ppermute(got, 'cand', mates))]
    ppermute x4 -> x5, starting transfers between devices: 8.91 us -> 9.1 us  [gather_over(): got.append(lax.ppermute(x, both, [(i, i ^ mask) for i in range(n)]))]
  transfers between devices with their start and end apart: 9 -> 10, of which waited for: 3 -> 4; matrix products, arithmetic and copies ran while one was open for 0% -> 0% of each run, Pallas kernels for 11% -> 13%
where the time goes in v2:
time: 26.9 us; the launch traced here: 26.7 us
  starting transfers between devices  11.9 us (44%)
  Pallas kernels  6.65 us (25%)
  waiting for transfers between devices  6.58 us (24%)
  between operations  1.53 us (6%)
    ppermute x5, starting transfers between devices, gather_over(): got.append(lax.ppermute(x, both, [(i, i ^ mask) for i in range(n)]))  9.1 us
    ppermute x2, waiting for transfers between devices, on_device(): lax.ppermute(piece, 'query', [(i, (i + shift) % n_query) for i in range(n...  3.07 us
    ppermute x5, waiting for transfers between devices, gather_over(): got.append(lax.ppermute(x, both, [(i, i ^ mask) for i in range(n)]))  2.6 us
    pallas_call x2, Pallas kernels, scores(): pl.pallas_call(functools.partial(scores_kernel, first, start, width), in_...  2.09 us
    ppermute x2, starting transfers between devices, on_device(): lax.ppermute(piece, 'query', [(i, (i + shift) % n_query) for i in range(n...  2.03 us
    pallas_call x1, Pallas kernels, start(): pl.pallas_call(functools.partial(start_kernel, share), in_specs=[pl.Block...  1.47 us
    pallas_call x1, Pallas kernels, totals(): pl.pallas_call(functools.partial(totals_kernel, start, width, len(before)...  1.32 us
    pallas_call x1, Pallas kernels, gains_of(): pl.pallas_call(functools.partial(gains_kernel, scale), in_specs=[VMEM] *...  1.07 us
  transfers between devices with their start and end apart: 10, of which 4 were waited for; matrix products, arithmetic and copies ran while one was open for 0% of the time, Pallas kernels for 13%

profile of v2, /device:TPU:0, one launch (start us, length us, event | category | flops | bytes accessed | tf_op | source)
XLA Modules:
  0.0 26.7 jit_solution(16563364985246411407)
XLA Ops:
  0.6 0.0 copy-start.1
  0.6 0.0 copy-start
  1.4 1.5 %start.1 = (bf16[1,32,128]{2,1,0:T(8,128)(2,1)S(1)}, bf16[64,2560]{1,0:T(8,128)(2,1)S(1)}, bf16[64,1536]{1,0:T(8,128)(2,1)S(1)}) custom-call(s32[1]{0:T(128)S(6)} %copy.13.pick_ids, bf16[1280,4096]{1,0:T(8,128)(2,1)} %pool.7, bf16[128,4096]{1,0:T(8,128)(2,1)} %refs_0_.1), custom_call_target="tpu_custom_call" | custom-call | bytes 41943040 | tf_op jit(solution)/shard_map/start/pallas_call | solution.py:78
  2.9 3.1 %collective-permute-start.4 = (bf16[1,32,128]{2,1,0:T(8,128)(2,1)S(1)}, bf16[1,32,128]{2,1,0:T(8,128)(2,1)S(1)}, u32[]{:S(2)}, u32[]{:S(2)}) collective-permute-start(bf16[1,32,128]{2,1,0:T(8,128)(2,1)S(1)} %get-tuple-element.13), channel_id=1, source_target_pairs={{0,1},{1,0},{2,3},{3,2},{4,5},{5,4},{6,7},{7,6},{8,9},{9,8},{10,11... | collective-permute-start | bytes 24584 | tf_op jit(solution)/shard_map/ppermute | solution.py:297
  6.0 0.1 collective-permute-start.2
  6.1 1.9 %collective-permute-start = (bf16[64,2560]{1,0:T(8,128)(2,1)S(1)}, bf16[64,2560]{1,0:T(8,128)(2,1)S(1)}, u32[]{:S(2)}, u32[]{:S(2)}) collective-permute-start(bf16[64,2560]{1,0:T(8,128)(2,1)S(1)} %get-tuple-element.9), channel_id=1, source_target_pairs={{0,1},{1,0},{2,3},{3,2},{4,5},{5,4},{6,7},{7,6},{8,9},{9,8},{10,11... | collective-permute-start | bytes 983048 | tf_op jit(solution)/shard_map/ppermute | solution.py:319
  8.0 0.0 collective-permute-done.4
  8.0 1.6 %collective-permute-start.5 = (bf16[2,32,128]{2,1,0:T(8,128)(2,1)S(1)}, bf16[2,32,128]{2,1,0:T(8,128)(2,1)S(1)}, u32[]{:S(2)}, u32[]{:S(2)}) collective-permute-start(bf16[2,32,128]{2,1,0:T(8,128)(2,1)S(1)} %pad_maximum_fusion), channel_id=1, source_target_pairs={{0,4},{1,5},{2,6},{3,7},{4,0},{5,1},{6,2},{7,3},{8,12},{9,13},{10,... | collective-permute-start | bytes 49160 | tf_op jit(solution)/shard_map/ppermute | solution.py:297
  9.6 2.2 %collective-permute-done.5 = bf16[2,32,128]{2,1,0:T(8,128)(2,1)S(1)} collective-permute-done((bf16[2,32,128]{2,1,0:T(8,128)(2,1)S(1)}, bf16[2,32,128]{2,1,0:T(8,128)(2,1)S(1)}, u32[]{:S(2)}, u32[]{:S(2)}) %collective-permute-start.5) | collective-permute-done | bytes 16416 | tf_op jit(solution)/shard_map/ppermute | solution.py:297
  11.8 3.7 %collective-permute-start.6 = (bf16[4,32,128]{2,1,0:T(8,128)(2,1)S(1)}, bf16[4,32,128]{2,1,0:T(8,128)(2,1)S(1)}, u32[]{:S(2)}, u32[]{:S(2)}) collective-permute-start(bf16[4,32,128]{2,1,0:T(8,128)(2,1)S(1)} %get-tuple-element.16), channel_id=1, source_target_pairs={{0,24},{1,25},{2,26},{3,27},{4,28},{5,29},{6,30},{7,31},{8,16},{9,... | collective-permute-start | bytes 98312 | tf_op jit(solution)/shard_map/ppermute | solution.py:297
  15.5 0.0 collective-permute-start.8
  15.5 0.8 %collective-permute-start.7 = (bf16[4,32,128]{2,1,0:T(8,128)(2,1)S(1)}, bf16[4,32,128]{2,1,0:T(8,128)(2,1)S(1)}, u32[]{:S(2)}, u32[]{:S(2)}) collective-permute-start(bf16[4,32,128]{2,1,0:T(8,128)(2,1)S(1)} %get-tuple-element.16), channel_id=1, source_target_pairs={{0,16},{1,17},{2,18},{3,19},{4,20},{5,21},{6,22},{7,23},{8,24},{9,... | collective-permute-start | bytes 98312 | tf_op jit(solution)/shard_map/ppermute | solution.py:297
  16.3 3.1 %collective-permute-done.refs_0_.refs_1_ = bf16[64,2560]{1,0:T(8,128)(2,1)S(1)} collective-permute-done((bf16[64,2560]{1,0:T(8,128)(2,1)S(1)}, bf16[64,2560]{1,0:T(8,128)(2,1)S(1)}, u32[]{:S(2)}, u32[]{:S(2)}) %collective-permute-start) | collective-permute-done | bytes 327712 | tf_op jit(solution)/shard_map/ppermute | solution.py:319
  19.4 0.0 collective-permute-start.1
  19.4 0.0 collective-permute-done.6
  19.4 0.0 collective-permute-done.2.refs_2_.refs_3_
  19.4 0.6 %collective-permute-start.3 = (bf16[64,1536]{1,0:T(8,128)(2,1)S(1)}, bf16[64,1536]{1,0:T(8,128)(2,1)S(1)}, u32[]{:S(2)}, u32[]{:S(2)}) collective-permute-start(bf16[64,1536]{1,0:T(8,128)(2,1)S(1)} %collective-permute-done.2.refs_2_.refs_3_), channel_id=1, source_target_pairs={{0,2},{2,0},{4,6},{6,4},{8,10},{10,8},{12,14},{14,12},{16,18},{18,... | collective-permute-start | bytes 589832 | tf_op jit(solution)/shard_map/ppermute | solution.py:326
  20.0 0.4 %collective-permute-done.7 = bf16[4,32,128]{2,1,0:T(8,128)(2,1)S(1)} collective-permute-done((bf16[4,32,128]{2,1,0:T(8,128)(2,1)S(1)}, bf16[4,32,128]{2,1,0:T(8,128)(2,1)S(1)}, u32[]{:S(2)}, u32[]{:S(2)}) %collective-permute-start.7) | collective-permute-done | bytes 32800 | tf_op jit(solution)/shard_map/ppermute | solution.py:297
  20.4 0.0 collective-permute-done.8
  20.4 0.9 %collective-permute-done.3.refs_3_.refs_4_ = bf16[64,1536]{1,0:T(8,128)(2,1)S(1)} collective-permute-done((bf16[64,1536]{1,0:T(8,128)(2,1)S(1)}, bf16[64,1536]{1,0:T(8,128)(2,1)S(1)}, u32[]{:S(2)}, u32[]{:S(2)}) %collective-permute-start.3) | collective-permute-done | bytes 196640 | tf_op jit(solution)/shard_map/ppermute | solution.py:326
  21.3 0.0 collective-permute-done.1.refs_1_.refs_2_
  21.3 0.0 copy-done.1
  21.3 0.7 %cover.1.refs_0_ = f32[1,256]{1,0:T(1,128)S(1)} custom-call(bf16[16,32,128]{2,1,0:T(8,128)(2,1)S(1)} %constant_dynamic-update-slice_fusion.3.picks, bf16[128,4096]{1,0:T(8,128)(2,1)S(1)} %copy-done.1, bf16[64,2560]{1,0:T(8,128)(2,1)S(1)} %collective-permute-done.refs_0_.refs_1_, bf16[64,2560]{1,0:T(8,128)(2,1)S(1)} %collective-permute-done.1.refs_1_.refs_2_, ...), custom_call_target="tpu_custom_call" | custom-call | flops 536870912 | bytes 2097152 | tf_op jit(solution)/shard_map/cover/pallas_call | solution.py:221
  22.0 0.2 collective-permute-start.9
  22.2 0.0 copy-done
  22.2 1.0 %scores.3.refs_1_ = f32[640,256]{1,0:T(8,128)S(1)} custom-call(bf16[1280,4096]{1,0:T(8,128)(2,1)S(1)} %copy-done, bf16[128,4096]{1,0:T(8,128)(2,1)S(1)} %copy-done.1, bf16[64,2560]{1,0:T(8,128)(2,1)S(1)} %collective-permute-done.refs_0_.refs_1_, bf16[64,2560]{1,0:T(8,128)(2,1)S(1)} %collective-permute-done.1.refs_1_.refs_2_), custom_call_target="tpu_custom_call" | custom-call | flops 838860800 | bytes 3276800 | tf_op jit(solution)/shard_map/scores/pallas_call | solution.py:125
  23.2 0.0 copy-start.2
  23.3 1.0 %scores.2.refs_0_ = f32[640,256]{1,0:T(8,128)S(1)} custom-call(bf16[1280,4096]{1,0:T(8,128)(2,1)S(1)} %copy-done, bf16[128,4096]{1,0:T(8,128)(2,1)S(1)} %copy-done.1, bf16[64,2560]{1,0:T(8,128)(2,1)S(1)} %collective-permute-done.refs_0_.refs_1_, bf16[64,2560]{1,0:T(8,128)(2,1)S(1)} %collective-permute-done.1.refs_1_.refs_2_), custom_call_target="tpu_custom_call" | custom-call | flops 838860800 | bytes 3276800 | tf_op jit(solution)/shard_map/scores/pallas_call | solution.py:125
  24.3 1.3 %totals.1 = (f32[1280,256]{1,0:T(8,128)S(1)}, f32[10,128]{1,0:T(8,128)S(1)}) custom-call(bf16[1280,4096]{1,0:T(8,128)(2,1)S(1)} %copy-done, bf16[128,4096]{1,0:T(8,128)(2,1)S(1)} %copy-done.1, f32[640,256]{1,0:T(8,128)S(1)} %scores.2.refs_0_, f32[640,256]{1,0:T(8,128)S(1)} %scores.3.refs_1_, bf16[64,1536]{1,0:T(8,128)(2,1)S(1)} %collective-permute-done.2.refs_2_.refs_3_, ...), custom_call_target="tpu_custom_call" | custom-call | flops 1006632960 | bytes 3932160 | tf_op jit(solution)/shard_map/totals/pallas_call | solution.py:168
  25.6 0.0 collective-permute-done.9.refs_1_
  25.6 0.0 copy-done.2
  25.7 1.1 %gains.1 = (f32[8,128]{1,0:T(8,128)}, f32[1,128]{1,0:T(1,128)}) custom-call(s32[8,128]{1,0:T(8,128)S(1)} %bitcast.3, f32[1280,256]{1,0:T(8,128)S(1)} %get-tuple-element.11.total, f32[10,128]{1,0:T(8,128)S(1)} %get-tuple-element.12.top, f32[1,256]{1,0:T(1,128)S(1)} %cover.1.refs_0_, f32[1,256]{1,0:T(1,128)S(1)} %collective-permute-done.9.refs_1_), custom_call_target="tpu_custom_call" | custom-call | tf_op jit(solution)/shard_map/gains/pallas_call | solution.py:260
  (7 shorter events, 0.1 us)
Async XLA Ops:
  0.6 20.7 %copy-start.1 = (bf16[128,4096]{1,0:T(8,128)(2,1)S(1)}, bf16[128,4096]{1,0:T(8,128)(2,1)}, u32[]{:S(2)}) copy-start(bf16[128,4096]{1,0:T(8,128)(2,1)} %refs_0_.1) | copy-start | bytes 3145732
  0.6 21.6 %copy-start = (bf16[1280,4096]{1,0:T(8,128)(2,1)S(1)}, bf16[1280,4096]{1,0:T(8,128)(2,1)}, u32[]{:S(2)}) copy-start(bf16[1280,4096]{1,0:T(8,128)(2,1)} %pool.7) | copy-start | bytes 31457284
  2.9 5.1 %collective-permute-start.4 = (bf16[1,32,128]{2,1,0:T(8,128)(2,1)S(1)}, bf16[1,32,128]{2,1,0:T(8,128)(2,1)S(1)}, u32[]{:S(2)}, u32[]{:S(2)}) collective-permute-start(bf16[1,32,128]{2,1,0:T(8,128)(2,1)S(1)} %get-tuple-element.13), channel_id=1, source_target_pairs={{0,1},{1,0},{2,3},{3,2},{4,5},{5,4},{6,7},{7,6},{8,9},{9,8},{10,11... | collective-permute-start | bytes 24584 | tf_op jit(solution)/shard_map/ppermute | solution.py:297
  6.0 13.4 %collective-permute-start.2 = (bf16[64,1536]{1,0:T(8,128)(2,1)S(1)}, bf16[64,1536]{1,0:T(8,128)(2,1)S(1)}, u32[]{:S(2)}, u32[]{:S(2)}) collective-permute-start(bf16[64,1536]{1,0:T(8,128)(2,1)S(1)} %get-tuple-element.10), channel_id=1, source_target_pairs={{0,1},{1,0},{2,3},{3,2},{4,5},{5,4},{6,7},{7,6},{8,9},{9,8},{10,11... | collective-permute-start | bytes 589832 | tf_op jit(solution)/shard_map/ppermute | solution.py:319
  6.1 13.3 %collective-permute-start = (bf16[64,2560]{1,0:T(8,128)(2,1)S(1)}, bf16[64,2560]{1,0:T(8,128)(2,1)S(1)}, u32[]{:S(2)}, u32[]{:S(2)}) collective-permute-start(bf16[64,2560]{1,0:T(8,128)(2,1)S(1)} %get-tuple-element.9), channel_id=1, source_target_pairs={{0,1},{1,0},{2,3},{3,2},{4,5},{5,4},{6,7},{7,6},{8,9},{9,8},{10,11... | collective-permute-start | bytes 983048 | tf_op jit(solution)/shard_map/ppermute | solution.py:319
  8.0 3.8 %collective-permute-start.5 = (bf16[2,32,128]{2,1,0:T(8,128)(2,1)S(1)}, bf16[2,32,128]{2,1,0:T(8,128)(2,1)S(1)}, u32[]{:S(2)}, u32[]{:S(2)}) collective-permute-start(bf16[2,32,128]{2,1,0:T(8,128)(2,1)S(1)} %pad_maximum_fusion), channel_id=1, source_target_pairs={{0,4},{1,5},{2,6},{3,7},{4,0},{5,1},{6,2},{7,3},{8,12},{9,13},{10,... | collective-permute-start | bytes 49160 | tf_op jit(solution)/shard_map/ppermute | solution.py:297
  11.8 7.5 %collective-permute-start.6 = (bf16[4,32,128]{2,1,0:T(8,128)(2,1)S(1)}, bf16[4,32,128]{2,1,0:T(8,128)(2,1)S(1)}, u32[]{:S(2)}, u32[]{:S(2)}) collective-permute-start(bf16[4,32,128]{2,1,0:T(8,128)(2,1)S(1)} %get-tuple-element.16), channel_id=1, source_target_pairs={{0,24},{1,25},{2,26},{3,27},{4,28},{5,29},{6,30},{7,31},{8,16},{9,... | collective-permute-start | bytes 98312 | tf_op jit(solution)/shard_map/ppermute | solution.py:297
  15.5 4.8 %collective-permute-start.8 = (bf16[4,32,128]{2,1,0:T(8,128)(2,1)S(1)}, bf16[4,32,128]{2,1,0:T(8,128)(2,1)S(1)}, u32[]{:S(2)}, u32[]{:S(2)}) collective-permute-start(bf16[4,32,128]{2,1,0:T(8,128)(2,1)S(1)} %get-tuple-element.16), channel_id=1, source_target_pairs={{0,8},{1,9},{2,10},{3,11},{4,12},{5,13},{6,14},{7,15},{8,0},{9,1},... | collective-permute-start | bytes 98312 | tf_op jit(solution)/shard_map/ppermute | solution.py:297
  15.5 4.8 %collective-permute-start.7 = (bf16[4,32,128]{2,1,0:T(8,128)(2,1)S(1)}, bf16[4,32,128]{2,1,0:T(8,128)(2,1)S(1)}, u32[]{:S(2)}, u32[]{:S(2)}) collective-permute-start(bf16[4,32,128]{2,1,0:T(8,128)(2,1)S(1)} %get-tuple-element.16), channel_id=1, source_target_pairs={{0,16},{1,17},{2,18},{3,19},{4,20},{5,21},{6,22},{7,23},{8,24},{9,... | collective-permute-start | bytes 98312 | tf_op jit(solution)/shard_map/ppermute | solution.py:297
  19.4 1.9 %collective-permute-start.1 = (bf16[64,2560]{1,0:T(8,128)(2,1)S(1)}, bf16[64,2560]{1,0:T(8,128)(2,1)S(1)}, u32[]{:S(2)}, u32[]{:S(2)}) collective-permute-start(bf16[64,2560]{1,0:T(8,128)(2,1)S(1)} %collective-permute-done.refs_0_.refs_1_), channel_id=1, source_target_pairs={{0,2},{2,0},{4,6},{6,4},{8,10},{10,8},{12,14},{14,12},{16,18},{18,... | collective-permute-start | bytes 983048 | tf_op jit(solution)/shard_map/ppermute | solution.py:326
  19.4 1.9 %collective-permute-start.3 = (bf16[64,1536]{1,0:T(8,128)(2,1)S(1)}, bf16[64,1536]{1,0:T(8,128)(2,1)S(1)}, u32[]{:S(2)}, u32[]{:S(2)}) collective-permute-start(bf16[64,1536]{1,0:T(8,128)(2,1)S(1)} %collective-permute-done.2.refs_2_.refs_3_), channel_id=1, source_target_pairs={{0,2},{2,0},{4,6},{6,4},{8,10},{10,8},{12,14},{14,12},{16,18},{18,... | collective-permute-start | bytes 589832 | tf_op jit(solution)/shard_map/ppermute | solution.py:326
  22.0 3.6 %collective-permute-start.9 = (f32[1,256]{1,0:T(1,128)S(1)}, f32[1,256]{1,0:T(1,128)S(1)}, u32[]{:S(2)}, u32[]{:S(2)}) collective-permute-start(f32[1,256]{1,0:T(1,128)S(1)} %cover.1.refs_0_), channel_id=1, source_target_pairs={{0,2},{2,0},{4,6},{6,4},{8,10},{10,8},{12,14},{14,12},{16,18},{18,... | collective-permute-start | bytes 3080 | tf_op jit(solution)/shard_map/ppermute | solution.py:341
  23.2 2.4 %copy-start.2 = (s32[1024]{0:T(1024)S(1)}, s32[1024]{0:T(1024)}, u32[]{:S(2)}) copy-start(s32[1024]{0:T(1024)} %param.5) | copy-start | bytes 12292

commit v3 on v2

--- a/solution.py
+++ b/solution.py
@@ -180,8 +180,8 @@
 
 
 def cover_kernel(groups, picks, *refs):
-    best, wide = refs[-2:]
-    refs = list(refs[:-2])
+    best, sent, wide = refs[-3:]
+    refs = list(refs[:-3])
     blocks = [
         [[refs.pop(0) for _ in range(n_pieces)] for _ in range(n_chunks)]
         for n_chunks, n_pieces in groups
@@ -210,7 +210,13 @@
                 at -= held
         term = dot(rows, jnp.concatenate(some, axis=0))
         total = term if total is None else total + term
-    best[...] = jnp.max(total, axis=0, keepdims=True)
+    found = jnp.max(total, axis=0, keepdims=True)
+    best[...] = found
+    count = blocks[0][0][0].shape[0]
+    turned = [found[:, :count]]
+    for at in range(count, found.shape[1], count):
+        turned.append(pltpu.roll(found[:, at : at + count], count // 2, 1))
+    sent[...] = jnp.concatenate(turned, axis=1)
 
 
 def cover_of(picks, blocks):
@@ -221,8 +227,8 @@
     return pl.pallas_call(
         functools.partial(cover_kernel, groups),
         in_specs=[VMEM] * (1 + len(flat)),
-        out_specs=VMEM,
-        out_shape=jax.ShapeDtypeStruct((1, count), jnp.float32),
+        out_specs=[VMEM, VMEM],
+        out_shape=[jax.ShapeDtypeStruct((1, count), jnp.float32)] * 2,
         scratch_shapes=[pltpu.VMEM((n_picks * cut, LANES), jnp.float32)],
         compiler_params=PARAMS,
         cost_estimate=cost(2 * LANES, count, cut * LANES),
@@ -235,11 +241,7 @@
     best = bests[0][...]
     count = cover.shape[1]
     if len(bests) == 2:
-        theirs = bests[1][...]
-        turned = [theirs[:, :count]]
-        for at in range(count, best.shape[1], count):
-            turned.append(pltpu.roll(theirs[:, at : at + count], count // 2, 1))
-        best = jnp.maximum(best, jnp.concatenate(turned, axis=1))
+        best = jnp.maximum(best, bests[1][...])
     cover[...] = best[:, :count] * scale
 
     keep = diagonal()
@@ -279,7 +281,7 @@
     rounds = [[bit] for bit in bits]
     if len(bits) > 1:
         low, high = bits[-2:]
-        rounds[-2:] = [[low | high, high, low]]
+        rounds[-2:] = [[low | high, low, high]]
     return rounds
 
 
@@ -336,9 +338,10 @@
     pieces = [p for block in blocks[1:] for p in block[1]]
     total, top = totals(pool, held, before, pieces, sent[0].shape[1])
 
-    bests = [cover_of(picks, blocks)]
+    best, turned = cover_of(picks, blocks)
+    bests = [best]
     if swapped:
-        bests.append(lax.ppermute(bests[0], "cand", mates))
+        bests.append(lax.ppermute(turned, "cand", mates))
     gains, cover = gains_of(
         bests, cand_ids.reshape(-1, LANES), total, top, queries.shape[0], scale
     )

time: 26.9 us -> 26.8 us (level)
  no operation moved by 1% of the time
where the time goes in v3:
time: 26.8 us; the launch traced here: 26.6 us
  starting transfers between devices  11.8 us (44%)
  Pallas kernels  6.62 us (25%)
  waiting for transfers between devices  6.58 us (25%)
  between operations  1.52 us (6%)
    ppermute x5, starting transfers between devices, gather_over(): got.append(lax.ppermute(x, both, [(i, i ^ mask) for i in range(n)]))  9.1 us
    ppermute x2, waiting for transfers between devices, on_device(): lax.ppermute(piece, 'query', [(i, (i + shift) % n_query) for i in range(n...  3.07 us
    ppermute x5, waiting for transfers between devices, gather_over(): got.append(lax.ppermute(x, both, [(i, i ^ mask) for i in range(n)]))  2.59 us
    pallas_call x2, Pallas kernels, scores(): pl.pallas_call(functools.partial(scores_kernel, first, start, width), in_...  2.09 us
    ppermute x2, starting transfers between devices, on_device(): lax.ppermute(piece, 'query', [(i, (i + shift) % n_query) for i in range(n...  2.03 us
    pallas_call x1, Pallas kernels, start(): pl.pallas_call(functools.partial(start_kernel, share), in_specs=[pl.Block...  1.47 us
    pallas_call x1, Pallas kernels, totals(): pl.pallas_call(functools.partial(totals_kernel, start, width, len(before)...  1.31 us
    pallas_call x1, Pallas kernels, gains_of(): pl.pallas_call(functools.partial(gains_kernel, scale), in_specs=[VMEM] *...  1 us
  transfers between devices with their start and end apart: 10, of which 4 were waited for; matrix products, arithmetic and copies ran while one was open for 0% of the time, Pallas kernels for 13%

profile of v3, /device:TPU:0, one launch (start us, length us, event | category | flops | bytes accessed | tf_op | source)
XLA Modules:
  0.0 26.6 jit_solution(13063153123550096583)
XLA Ops:
  0.6 0.0 copy-start.1
  0.6 0.0 copy-start
  1.4 1.5 %start.1 = (bf16[1,32,128]{2,1,0:T(8,128)(2,1)S(1)}, bf16[64,2560]{1,0:T(8,128)(2,1)S(1)}, bf16[64,1536]{1,0:T(8,128)(2,1)S(1)}) custom-call(s32[1]{0:T(128)S(6)} %copy.13.pick_ids, bf16[1280,4096]{1,0:T(8,128)(2,1)} %pool.7, bf16[128,4096]{1,0:T(8,128)(2,1)} %refs_0_.1), custom_call_target="tpu_custom_call" | custom-call | bytes 41943040 | tf_op jit(solution)/shard_map/start/pallas_call | solution.py:78
  2.9 3.1 %collective-permute-start.4 = (bf16[1,32,128]{2,1,0:T(8,128)(2,1)S(1)}, bf16[1,32,128]{2,1,0:T(8,128)(2,1)S(1)}, u32[]{:S(2)}, u32[]{:S(2)}) collective-permute-start(bf16[1,32,128]{2,1,0:T(8,128)(2,1)S(1)} %get-tuple-element.15), channel_id=1, source_target_pairs={{0,1},{1,0},{2,3},{3,2},{4,5},{5,4},{6,7},{7,6},{8,9},{9,8},{10,11... | collective-permute-start | bytes 24584 | tf_op jit(solution)/shard_map/ppermute | solution.py:299
  6.0 0.1 collective-permute-start.2
  6.1 1.9 %collective-permute-start = (bf16[64,2560]{1,0:T(8,128)(2,1)S(1)}, bf16[64,2560]{1,0:T(8,128)(2,1)S(1)}, u32[]{:S(2)}, u32[]{:S(2)}) collective-permute-start(bf16[64,2560]{1,0:T(8,128)(2,1)S(1)} %get-tuple-element.11), channel_id=1, source_target_pairs={{0,1},{1,0},{2,3},{3,2},{4,5},{5,4},{6,7},{7,6},{8,9},{9,8},{10,11... | collective-permute-start | bytes 983048 | tf_op jit(solution)/shard_map/ppermute | solution.py:321
  8.0 0.0 collective-permute-done.4
  8.0 1.6 %collective-permute-start.5 = (bf16[2,32,128]{2,1,0:T(8,128)(2,1)S(1)}, bf16[2,32,128]{2,1,0:T(8,128)(2,1)S(1)}, u32[]{:S(2)}, u32[]{:S(2)}) collective-permute-start(bf16[2,32,128]{2,1,0:T(8,128)(2,1)S(1)} %pad_maximum_fusion), channel_id=1, source_target_pairs={{0,4},{1,5},{2,6},{3,7},{4,0},{5,1},{6,2},{7,3},{8,12},{9,13},{10,... | collective-permute-start | bytes 49160 | tf_op jit(solution)/shard_map/ppermute | solution.py:299
  9.6 2.2 %collective-permute-done.5 = bf16[2,32,128]{2,1,0:T(8,128)(2,1)S(1)} collective-permute-done((bf16[2,32,128]{2,1,0:T(8,128)(2,1)S(1)}, bf16[2,32,128]{2,1,0:T(8,128)(2,1)S(1)}, u32[]{:S(2)}, u32[]{:S(2)}) %collective-permute-start.5) | collective-permute-done | bytes 16416 | tf_op jit(solution)/shard_map/ppermute | solution.py:299
  11.8 3.7 %collective-permute-start.6 = (bf16[4,32,128]{2,1,0:T(8,128)(2,1)S(1)}, bf16[4,32,128]{2,1,0:T(8,128)(2,1)S(1)}, u32[]{:S(2)}, u32[]{:S(2)}) collective-permute-start(bf16[4,32,128]{2,1,0:T(8,128)(2,1)S(1)} %get-tuple-element.20), channel_id=1, source_target_pairs={{0,24},{1,25},{2,26},{3,27},{4,28},{5,29},{6,30},{7,31},{8,16},{9,... | collective-permute-start | bytes 98312 | tf_op jit(solution)/shard_map/ppermute | solution.py:299
  15.5 0.0 collective-permute-start.8
  15.5 0.8 %collective-permute-start.7 = (bf16[4,32,128]{2,1,0:T(8,128)(2,1)S(1)}, bf16[4,32,128]{2,1,0:T(8,128)(2,1)S(1)}, u32[]{:S(2)}, u32[]{:S(2)}) collective-permute-start(bf16[4,32,128]{2,1,0:T(8,128)(2,1)S(1)} %get-tuple-element.20), channel_id=1, source_target_pairs={{0,8},{1,9},{2,10},{3,11},{4,12},{5,13},{6,14},{7,15},{8,0},{9,1},... | collective-permute-start | bytes 98312 | tf_op jit(solution)/shard_map/ppermute | solution.py:299
  16.3 3.1 %collective-permute-done.refs_0_.refs_1_ = bf16[64,2560]{1,0:T(8,128)(2,1)S(1)} collective-permute-done((bf16[64,2560]{1,0:T(8,128)(2,1)S(1)}, bf16[64,2560]{1,0:T(8,128)(2,1)S(1)}, u32[]{:S(2)}, u32[]{:S(2)}) %collective-permute-start) | collective-permute-done | bytes 327712 | tf_op jit(solution)/shard_map/ppermute | solution.py:321
  19.4 0.0 collective-permute-start.1
  19.4 0.0 collective-permute-done.6
  19.4 0.0 collective-permute-done.2.refs_2_.refs_3_
  19.4 0.6 %collective-permute-start.3 = (bf16[64,1536]{1,0:T(8,128)(2,1)S(1)}, bf16[64,1536]{1,0:T(8,128)(2,1)S(1)}, u32[]{:S(2)}, u32[]{:S(2)}) collective-permute-start(bf16[64,1536]{1,0:T(8,128)(2,1)S(1)} %collective-permute-done.2.refs_2_.refs_3_), channel_id=1, source_target_pairs={{0,2},{2,0},{4,6},{6,4},{8,10},{10,8},{12,14},{14,12},{16,18},{18,... | collective-permute-start | bytes 589832 | tf_op jit(solution)/shard_map/ppermute | solution.py:328
  20.0 0.0 collective-permute-done.7
  20.0 0.4 %collective-permute-done.8 = bf16[4,32,128]{2,1,0:T(8,128)(2,1)S(1)} collective-permute-done((bf16[4,32,128]{2,1,0:T(8,128)(2,1)S(1)}, bf16[4,32,128]{2,1,0:T(8,128)(2,1)S(1)}, u32[]{:S(2)}, u32[]{:S(2)}) %collective-permute-start.8) | collective-permute-done | bytes 32800 | tf_op jit(solution)/shard_map/ppermute | solution.py:299
  20.4 0.9 %collective-permute-done.3.refs_3_.refs_4_ = bf16[64,1536]{1,0:T(8,128)(2,1)S(1)} collective-permute-done((bf16[64,1536]{1,0:T(8,128)(2,1)S(1)}, bf16[64,1536]{1,0:T(8,128)(2,1)S(1)}, u32[]{:S(2)}, u32[]{:S(2)}) %collective-permute-start.3) | collective-permute-done | bytes 196640 | tf_op jit(solution)/shard_map/ppermute | solution.py:328
  21.3 0.0 collective-permute-done.1.refs_1_.refs_2_
  21.3 0.0 copy-done.1
  21.3 0.8 %cover.1 = (f32[1,256]{1,0:T(1,128)S(1)}, f32[1,256]{1,0:T(1,128)S(1)}) custom-call(bf16[16,32,128]{2,1,0:T(8,128)(2,1)S(1)} %constant_dynamic-update-slice_fusion.3.picks, bf16[128,4096]{1,0:T(8,128)(2,1)S(1)} %copy-done.1, bf16[64,2560]{1,0:T(8,128)(2,1)S(1)} %collective-permute-done.refs_0_.refs_1_, ...), custom_call_target="tpu_custom_call" | custom-call | flops 536870912 | bytes 2097152 | tf_op jit(solution)/shard_map/cover/pallas_call | solution.py:227
  22.0 0.1 collective-permute-start.9
  22.2 0.0 copy-done
  22.2 1.0 %scores.3.refs_1_ = f32[640,256]{1,0:T(8,128)S(1)} custom-call(bf16[1280,4096]{1,0:T(8,128)(2,1)S(1)} %copy-done, bf16[128,4096]{1,0:T(8,128)(2,1)S(1)} %copy-done.1, bf16[64,2560]{1,0:T(8,128)(2,1)S(1)} %collective-permute-done.refs_0_.refs_1_, bf16[64,2560]{1,0:T(8,128)(2,1)S(1)} %collective-permute-done.1.refs_1_.refs_2_), custom_call_target="tpu_custom_call" | custom-call | flops 838860800 | bytes 3276800 | tf_op jit(solution)/shard_map/scores/pallas_call | solution.py:125
  23.2 0.0 copy-start.2
  23.3 1.0 %scores.2.refs_0_ = f32[640,256]{1,0:T(8,128)S(1)} custom-call(bf16[1280,4096]{1,0:T(8,128)(2,1)S(1)} %copy-done, bf16[128,4096]{1,0:T(8,128)(2,1)S(1)} %copy-done.1, bf16[64,2560]{1,0:T(8,128)(2,1)S(1)} %collective-permute-done.refs_0_.refs_1_, bf16[64,2560]{1,0:T(8,128)(2,1)S(1)} %collective-permute-done.1.refs_1_.refs_2_), custom_call_target="tpu_custom_call" | custom-call | flops 838860800 | bytes 3276800 | tf_op jit(solution)/shard_map/scores/pallas_call | solution.py:125
  24.3 1.3 %totals.1 = (f32[1280,256]{1,0:T(8,128)S(1)}, f32[10,128]{1,0:T(8,128)S(1)}) custom-call(bf16[1280,4096]{1,0:T(8,128)(2,1)S(1)} %copy-done, bf16[128,4096]{1,0:T(8,128)(2,1)S(1)} %copy-done.1, f32[640,256]{1,0:T(8,128)S(1)} %scores.2.refs_0_, f32[640,256]{1,0:T(8,128)S(1)} %scores.3.refs_1_, bf16[64,1536]{1,0:T(8,128)(2,1)S(1)} %collective-permute-done.2.refs_2_.refs_3_, ...), custom_call_target="tpu_custom_call" | custom-call | flops 1006632960 | bytes 3932160 | tf_op jit(solution)/shard_map/totals/pallas_call | solution.py:168
  25.6 0.0 collective-permute-done.9.refs_1_
  25.6 0.0 copy-done.2
  25.6 1.0 %gains.1 = (f32[8,128]{1,0:T(8,128)}, f32[1,128]{1,0:T(1,128)}) custom-call(s32[8,128]{1,0:T(8,128)S(1)} %bitcast.3, f32[1280,256]{1,0:T(8,128)S(1)} %get-tuple-element.13.total, f32[10,128]{1,0:T(8,128)S(1)} %get-tuple-element.14.top, f32[1,256]{1,0:T(1,128)S(1)} %get-tuple-element.16.refs_0_, f32[1,256]{1,0:T(1,128)S(1)} %collective-permute-done.9.refs_1_), custom_call_target="tpu_custom_call" | custom-call | tf_op jit(solution)/shard_map/gains/pallas_call | solution.py:262
  (7 shorter events, 0.1 us)
Async XLA Ops:
  0.6 20.7 %copy-start.1 = (bf16[128,4096]{1,0:T(8,128)(2,1)S(1)}, bf16[128,4096]{1,0:T(8,128)(2,1)}, u32[]{:S(2)}) copy-start(bf16[128,4096]{1,0:T(8,128)(2,1)} %refs_0_.1) | copy-start | bytes 3145732
  0.6 21.5 %copy-start = (bf16[1280,4096]{1,0:T(8,128)(2,1)S(1)}, bf16[1280,4096]{1,0:T(8,128)(2,1)}, u32[]{:S(2)}) copy-start(bf16[1280,4096]{1,0:T(8,128)(2,1)} %pool.7) | copy-start | bytes 31457284
  2.9 5.1 %collective-permute-start.4 = (bf16[1,32,128]{2,1,0:T(8,128)(2,1)S(1)}, bf16[1,32,128]{2,1,0:T(8,128)(2,1)S(1)}, u32[]{:S(2)}, u32[]{:S(2)}) collective-permute-start(bf16[1,32,128]{2,1,0:T(8,128)(2,1)S(1)} %get-tuple-element.15), channel_id=1, source_target_pairs={{0,1},{1,0},{2,3},{3,2},{4,5},{5,4},{6,7},{7,6},{8,9},{9,8},{10,11... | collective-permute-start | bytes 24584 | tf_op jit(solution)/shard_map/ppermute | solution.py:299
  6.0 13.4 %collective-permute-start.2 = (bf16[64,1536]{1,0:T(8,128)(2,1)S(1)}, bf16[64,1536]{1,0:T(8,128)(2,1)S(1)}, u32[]{:S(2)}, u32[]{:S(2)}) collective-permute-start(bf16[64,1536]{1,0:T(8,128)(2,1)S(1)} %get-tuple-element.12), channel_id=1, source_target_pairs={{0,1},{1,0},{2,3},{3,2},{4,5},{5,4},{6,7},{7,6},{8,9},{9,8},{10,11... | collective-permute-start | bytes 589832 | tf_op jit(solution)/shard_map/ppermute | solution.py:321
  6.1 13.3 %collective-permute-start = (bf16[64,2560]{1,0:T(8,128)(2,1)S(1)}, bf16[64,2560]{1,0:T(8,128)(2,1)S(1)}, u32[]{:S(2)}, u32[]{:S(2)}) collective-permute-start(bf16[64,2560]{1,0:T(8,128)(2,1)S(1)} %get-tuple-element.11), channel_id=1, source_target_pairs={{0,1},{1,0},{2,3},{3,2},{4,5},{5,4},{6,7},{7,6},{8,9},{9,8},{10,11... | collective-permute-start | bytes 983048 | tf_op jit(solution)/shard_map/ppermute | solution.py:321
  8.0 3.8 %collective-permute-start.5 = (bf16[2,32,128]{2,1,0:T(8,128)(2,1)S(1)}, bf16[2,32,128]{2,1,0:T(8,128)(2,1)S(1)}, u32[]{:S(2)}, u32[]{:S(2)}) collective-permute-start(bf16[2,32,128]{2,1,0:T(8,128)(2,1)S(1)} %pad_maximum_fusion), channel_id=1, source_target_pairs={{0,4},{1,5},{2,6},{3,7},{4,0},{5,1},{6,2},{7,3},{8,12},{9,13},{10,... | collective-permute-start | bytes 49160 | tf_op jit(solution)/shard_map/ppermute | solution.py:299
  11.8 7.5 %collective-permute-start.6 = (bf16[4,32,128]{2,1,0:T(8,128)(2,1)S(1)}, bf16[4,32,128]{2,1,0:T(8,128)(2,1)S(1)}, u32[]{:S(2)}, u32[]{:S(2)}) collective-permute-start(bf16[4,32,128]{2,1,0:T(8,128)(2,1)S(1)} %get-tuple-element.20), channel_id=1, source_target_pairs={{0,24},{1,25},{2,26},{3,27},{4,28},{5,29},{6,30},{7,31},{8,16},{9,... | collective-permute-start | bytes 98312 | tf_op jit(solution)/shard_map/ppermute | solution.py:299
  15.5 4.8 %collective-permute-start.8 = (bf16[4,32,128]{2,1,0:T(8,128)(2,1)S(1)}, bf16[4,32,128]{2,1,0:T(8,128)(2,1)S(1)}, u32[]{:S(2)}, u32[]{:S(2)}) collective-permute-start(bf16[4,32,128]{2,1,0:T(8,128)(2,1)S(1)} %get-tuple-element.20), channel_id=1, source_target_pairs={{0,16},{1,17},{2,18},{3,19},{4,20},{5,21},{6,22},{7,23},{8,24},{9,... | collective-permute-start | bytes 98312 | tf_op jit(solution)/shard_map/ppermute | solution.py:299
  15.5 4.4 %collective-permute-start.7 = (bf16[4,32,128]{2,1,0:T(8,128)(2,1)S(1)}, bf16[4,32,128]{2,1,0:T(8,128)(2,1)S(1)}, u32[]{:S(2)}, u32[]{:S(2)}) collective-permute-start(bf16[4,32,128]{2,1,0:T(8,128)(2,1)S(1)} %get-tuple-element.20), channel_id=1, source_target_pairs={{0,8},{1,9},{2,10},{3,11},{4,12},{5,13},{6,14},{7,15},{8,0},{9,1},... | collective-permute-start | bytes 98312 | tf_op jit(solution)/shard_map/ppermute | solution.py:299
  19.4 1.9 %collective-permute-start.1 = (bf16[64,2560]{1,0:T(8,128)(2,1)S(1)}, bf16[64,2560]{1,0:T(8,128)(2,1)S(1)}, u32[]{:S(2)}, u32[]{:S(2)}) collective-permute-start(bf16[64,2560]{1,0:T(8,128)(2,1)S(1)} %collective-permute-done.refs_0_.refs_1_), channel_id=1, source_target_pairs={{0,2},{2,0},{4,6},{6,4},{8,10},{10,8},{12,14},{14,12},{16,18},{18,... | collective-permute-start | bytes 983048 | tf_op jit(solution)/shard_map/ppermute | solution.py:328
  19.4 1.9 %collective-permute-start.3 = (bf16[64,1536]{1,0:T(8,128)(2,1)S(1)}, bf16[64,1536]{1,0:T(8,128)(2,1)S(1)}, u32[]{:S(2)}, u32[]{:S(2)}) collective-permute-start(bf16[64,1536]{1,0:T(8,128)(2,1)S(1)} %collective-permute-done.2.refs_2_.refs_3_), channel_id=1, source_target_pairs={{0,2},{2,0},{4,6},{6,4},{8,10},{10,8},{12,14},{14,12},{16,18},{18,... | collective-permute-start | bytes 589832 | tf_op jit(solution)/shard_map/ppermute | solution.py:328
  22.0 3.6 %collective-permute-start.9 = (f32[1,256]{1,0:T(1,128)S(1)}, f32[1,256]{1,0:T(1,128)S(1)}, u32[]{:S(2)}, u32[]{:S(2)}) collective-permute-start(f32[1,256]{1,0:T(1,128)S(1)} %get-tuple-element.17), channel_id=1, source_target_pairs={{0,2},{2,0},{4,6},{6,4},{8,10},{10,8},{12,14},{14,12},{16,18},{18,... | collective-permute-start | bytes 3080 | tf_op jit(solution)/shard_map/ppermute | solution.py:344
  23.2 2.4 %copy-start.2 = (s32[1024]{0:T(1024)S(1)}, s32[1024]{0:T(1024)}, u32[]{:S(2)}) copy-start(s32[1024]{0:T(1024)} %param.5) | copy-start | bytes 12292
